TPU v7x, 256 devices: a whole 4x4x8 slice. The times are simulated.
256 devices in a mesh: code: 32 (over y, z), dp: 8 (over x, core).
Axes of the slice: x: 4, y: 4, z: 8, core: 2. Of those that a mesh axis runs over, the one named last changes fastest.
Arguments:
- codebook: bfloat16 [262144, 768], P(('code', 'dp')), may hold values from -6 to 6
- weight_in: bfloat16 [768, 1024], replicated, may hold values from -0.21875 to 0.21875
- bias_in: float32 [1024], replicated, may hold values from -3 to 3
- weight_out: bfloat16 [1024, 256], replicated, may hold values from -0.1875 to 0.1875
- bias_out: float32 [256], replicated, may hold values from -3 to 3
- latents: float32 [262144, 256], P(('code', 'dp')), may hold values from -6 to 6
- cotangent: float32 [262144, 256], P(('code', 'dp')), may hold values from -6 to 6
- code_owner: int32 [262144, 1], P(('code', 'dp')), may hold values from 0 to 255; in each aligned block of 1024 rows (0 to 1023, 1024 to 2047, ...) at most 8 rows name the same one
- code_row: int32 [262144], P(('code', 'dp')), may hold values from 0 to 1023
Outputs:
- latent_grad: float32 [262144, 256], P(('code', 'dp'))
- grad_weight_in: float32 [768, 1024], replicated
- grad_bias_in: float32 [1024], replicated
- grad_weight_out: float32 [1024, 256], replicated
- grad_bias_out: float32 [256], replicated
Inputs may be any that keep to these rules, and one draw needn't show every extreme that they name: In the rows of one device no owner is named by more than 8 rows, a bound that some block reaches; a latent's code is code_owner * 1024 + code_row.
All inputs are finite; a program needn't handle non-finite values.
Results may differ from a plain program's by a relative error of at most 0.0023.
Values sent between devices are 32-bit elements; how exact they have to be, the bound alone decides.
A program may use at most 128 MiB of HBM per device.

v0:
```python
import jax
import jax.numpy as jnp
from jax import lax
from jax.sharding import PartitionSpec as P

scale_gelu = 0.7978845608028654
cubic_term = 0.044715


def in_blocks(array, dim, size):
    before, after = (array.shape[:dim], array.shape[dim + 1 :])
    return jnp.moveaxis(array.reshape(*before, size, -1, *after), dim, 0)


def in_order(tiles, dim):
    shape = list(tiles.shape[1:])
    shape[dim] *= tiles.shape[0]
    return jnp.moveaxis(tiles, 0, dim).reshape(shape)


def exchange_both(array, axis, axes, splits, concats):
    sizes = [lax.axis_size(a) for a in axes]
    tiles = in_blocks(array, splits[0], sizes[0])
    tiles = jnp.moveaxis(in_blocks(tiles, splits[1] + 1, sizes[1]), 0, 1)
    inside = tiles.shape[2:]
    tiles = tiles.reshape(-1, *inside)
    tiles = lax.all_to_all(tiles, axis, split_axis=0, concat_axis=0, tiled=True)
    tiles = in_order(tiles.reshape(*sizes, *inside), concats[0] + 1)
    return in_order(tiles, concats[1])


def gelu_value(x):
    inner = scale_gelu * (x + cubic_term * x * x * x)
    return 0.5 * x * (1.0 + jnp.tanh(inner))


def gelu_slope(x):
    tangent = jnp.tanh(scale_gelu * (x + cubic_term * x * x * x))
    return 0.5 * (1.0 + tangent) + 0.5 * x * (1.0 - tangent * tangent) * scale_gelu * (
        1.0 + 3.0 * cubic_term * x * x
    )


def per_device(
    codebook, weight_in, bias_in, weight_out, bias_out, latents, cotangent, code_owner, code_row
):
    preact = jnp.dot(codebook, weight_in, preferred_element_type=jnp.float32) + bias_in
    hidden = gelu_value(preact).astype(jnp.bfloat16)
    projected = jnp.dot(hidden, weight_out, preferred_element_type=jnp.float32) + bias_out
    n_code = lax.axis_size("code")
    n_data = lax.axis_size("dp")
    devices = n_code * n_data
    owners = code_owner[:, 0]
    count = owners.shape[0]
    width = latents.shape[1]
    capacity = max(2, 2 * count // devices)
    position = jnp.arange(count, dtype=jnp.int32)
    same = (owners[:, None] == owners[None, :]) & (position[None, :] < position[:, None])
    ranks = jnp.sum(same.astype(jnp.int32), axis=1)
    slots = owners * capacity + ranks
    wanted = jnp.full((devices * capacity,), -1, jnp.int32).at[slots].set(code_row)
    wanted = exchange_both(
        wanted.reshape(n_code, n_data, capacity), ("code", "dp"), ("code", "dp"), (0, 1), (0, 1)
    )
    valid = wanted >= 0
    row_ids = jnp.maximum(wanted, 0).reshape(-1)
    picked = jnp.take(projected, row_ids, axis=0).reshape(n_code, n_data, capacity, width)
    picked = jnp.where(valid[..., None], picked, 0.0)
    answers = exchange_both(picked, ("code", "dp"), ("code", "dp"), (0, 1), (0, 1))
    chosen = jnp.take(answers.reshape(devices * capacity, width), slots, axis=0)
    residual = chosen - latents
    latent_grad = cotangent - 0.25 * residual
    outgoing = (
        jnp.zeros((devices * capacity, width), jnp.float32).at[slots].set(cotangent + residual)
    )
    incoming = exchange_both(
        outgoing.reshape(n_code, n_data, capacity, width),
        ("code", "dp"),
        ("code", "dp"),
        (0, 1),
        (0, 1),
    )
    code_grad = jax.ops.segment_sum(
        incoming.reshape(devices * capacity, width), row_ids, num_segments=projected.shape[0]
    )
    code_low = code_grad.astype(jnp.bfloat16)
    gw_out = lax.dot_general(
        hidden, code_low, (((0,), (0,)), ((), ())), preferred_element_type=jnp.float32
    )
    back = lax.dot_general(
        code_low, weight_out, (((1,), (1,)), ((), ())), preferred_element_type=jnp.float32
    )
    preact_grad = (back * gelu_slope(preact)).astype(jnp.bfloat16)
    gb_in = jnp.sum(preact_grad.astype(jnp.float32), axis=0)
    gw_in = lax.dot_general(
        codebook, preact_grad, (((0,), (0,)), ((), ())), preferred_element_type=jnp.float32
    )
    gb_out = jnp.sum(code_grad, axis=0)
    gw_in, gb_in, gw_out, gb_out = lax.psum((gw_in, gb_in, gw_out, gb_out), ("code", "dp"))
    return (latent_grad, gw_in, gb_in, gw_out, gb_out)


def solution(mesh):
    placed = (
        P(("code", "dp"), None),
        P(),
        P(),
        P(),
        P(),
        P(("code", "dp"), None),
        P(("code", "dp"), None),
        P(("code", "dp"), None),
        P(("code", "dp")),
    )
    return jax.shard_map(
        per_device,
        mesh=mesh,
        in_specs=placed,
        out_specs=(P(("code", "dp"), None), P(), P(), P(), P()),
        check_vma=False,
    )
```

profile of v0, /device:TPU:1, one launch (start us, length us, event | category | flops | bytes accessed | tf_op | source)
XLA Modules:
  0.0 491.4 jit_solution(8340644630260382695)
XLA Ops:
  7.2 1.3 convert_reduce_fusion.1
  8.5 0.7 and_reduce_fusion
  9.2 4.5 scatter_custom_fusion
  13.7 0.8 reshape_transpose_transpose_reshape_reshape_reshape.6
  14.5 15.6 %all-to-all-start = ((s32[256,1,1,8]{3,2,1,0:T(1,128)}), s32[256,1,1,8]{3,2,1,0:T(1,128)S(1)}, u32[]{:S(2)}, u32[]{:S(2)}) async-start(s32[256,1,1,8]{3,2,1,0:T(1,128)} %bitcast.3), calls=%async_computation | async-start | bytes 262144 | tf_op jit(solution)/shard_map/all_to_all | solution.py:27
  30.2 5.9 %multiply_convert_fusion = (bf16[1024,1024]{1,0:T(8,128)(2,1)S(1)}, f32[1024,1024]{1,0:T(8,128)}) fusion(f32[1024]{0:T(1024)} %param.11, bf16[1024,768]{1,0:T(8,128)(2,1)S(1)} %copy-done, bf16[768,1024]{1,0:T(8,128)(2,1)} %param.10), kind=kOutput, calls=%fused_computation.15 | convolution fusion | flops 1621098496 | bytes 9441280 | tf_op jit(solution)/shard_map/dot_general | solution.py:47
  36.1 1.3 copy-done.6
  37.4 0.7 convolution_add_fusion
  38.1 4.7 all-to-all-done
  42.9 0.2 broadcast_compare_fusion
  43.0 0.1 copy.30
  43.1 0.1 broadcast_maximum_fusion
  43.3 0.1 reshape.110
  43.4 0.1 reshape.105
  43.5 0.2 copy.34
  43.7 8.6 %gather_fusion = f32[2048,256]{1,0:T(8,128)} fusion(f32[1024,256]{1,0:T(8,128)S(1)} %convolution_add_fusion, s32[2048]{0:T(1024)S(1)} %broadcast_clamp_fusion), kind=kCustom, calls=%fused_computation | custom fusion | bytes 4202496 | tf_op jit(solution)/shard_map/jit(_take)/gather | solution.py:67
  52.3 4.2 fusion.10
  56.5 10.0 %all-to-all-start.1 = ((f32[256,1,1,8,256]{4,3,2,1,0:T(8,128)}), f32[256,1,1,8,256]{4,3,2,1,0:T(8,128)}, u32[]{:S(2)}, u32[]{:S(2)}) async-start(f32[256,1,1,8,256]{4,3,2,1,0:T(8,128)} %fusion.10), calls=%async_computation.1 | async-start | bytes 4194304 | tf_op jit(solution)/shard_map/all_to_all | solution.py:27
  66.6 52.4 %all-to-all-done.1 = f32[256,1,1,8,256]{4,3,2,1,0:T(8,128)} async-done(((f32[256,1,1,8,256]{4,3,2,1,0:T(8,128)}), f32[256,1,1,8,256]{4,3,2,1,0:T(8,128)}, u32[]{:S(2)}, u32[]{:S(2)}) %all-to-all-start.1) | async-done | bytes 2097184 | tf_op jit(solution)/shard_map/all_to_all | solution.py:27
  119.0 5.1 %gather_fusion.1 = f32[1024,256]{1,0:T(8,128)S(1)} fusion(f32[2048,256]{1,0:T(8,128)} %bitcast.22, s32[1024]{0:T(1024)S(1)} %broadcast_clamp_fusion.1), kind=kCustom, calls=%fused_computation.1 | custom fusion | bytes 2101248 | tf_op jit(solution)/shard_map/jit(_take)/gather | solution.py:70
  124.0 7.5 %scatter_custom_fusion.1 = f32[2048,256]{1,0:T(8,128)} fusion(s32[1024]{0:T(1024)S(1)} %bitcast.77, f32[1024,256]{1,0:T(8,128)} %param.15, f32[]{:T(128)} %constant.32.clone.1, f32[1024,256]{1,0:T(8,128)} %param.14, f32[1024,256]{1,0:T(8,128)S(1)} %gather_fusion.1, f32[]{:T(128)} %constant.31.clone.1, pred[1024]{0:T(1024)(128)(4,1)S(1)} %get-tuple-element.39), kind=kCustom, calls=%fused_computation.25 | custom fusion | flops 786432 | bytes 5243912 | tf_op jit(solution)/shard_map/scatter | solution.py:74
  131.5 60.8 %all_to_all.15 = f32[256,1,1,8,256]{4,3,2,1,0:T(8,128)} all-to-all(f32[256,1,1,8,256]{4,3,2,1,0:T(8,128)} %bitcast.70), channel_id=1, replica_groups=mesh['code'=32,'dp'=8] {'code','dp'}, dimensions={0} | all-to-all | bytes 4194304 | tf_op jit(solution)/shard_map/all_to_all | solution.py:27
  192.3 13.1 %scatter_custom_fusion.2 = f32[1024,256]{1,0:T(8,128)} fusion(s32[2048]{0:T(1024)S(1)} %reshape.110, f32[256,1,1,8,256]{4,3,2,1,0:T(8,128)} %all_to_all.15, f32[]{:T(128)} %constant.32.clone.1), kind=kCustom, calls=%fused_computation.19 | custom fusion | flops 524288 | bytes 3145732 | tf_op jit(solution)/shard_map/scatter-add | solution.py:83
  205.4 3.8 fusion.15
  209.1 3.2 convert_reduce_fusion
  212.4 3.6 convolution_bitcast_fusion
  216.0 2.8 multiply_subtract_fusion
  218.7 1.4 reduce_sum.32
  220.1 74.2 %all-reduce = (f32[1024]{0:T(1024)}, f32[256]{0:T(256)}) all-reduce(f32[1024]{0:T(1024)S(1)} %get-tuple-element.43, f32[256]{0:T(256)S(1)} %reduce_sum.32), channel_id=1, replica_groups=mesh['code'=32,'dp'=8] {'code','dp'}, use_global_device_ids=true, to_apply=%region_6.7 | all-reduce | flops 1280 | bytes 10240 | tf_op jit(solution)/shard_map/psum | solution.py:99
  294.2 185.8 %all-reduce.4.cloned.1.call-done = (f32[768,1024]{0,1:T(8,128)}, f32[1024,256]{1,0:T(8,128)}) async-done(((f32[768,1024]{0,1:T(8,128)}, f32[1024,256]{1,0:T(8,128)}), (f32[768,1024]{0,1:T(8,128)}, f32[1024,256]{1,0:T(8,128)})) %all-reduce.4.cloned.1.call-update) | async-done | bytes 4194320 | tf_op jit(solution)/shard_map/psum | solution.py:99
  480.0 3.6 copy.33
  483.6 1.0 copy.37
  (20 shorter events, 0.1 us)
Async XLA Ops:
  7.2 23.0 %copy-start = (bf16[1024,768]{1,0:T(8,128)(2,1)S(1)}, bf16[1024,768]{1,0:T(8,128)(2,1)}, u32[]{:S(2)}) copy-start(bf16[1024,768]{1,0:T(8,128)(2,1)} %param.9) | copy-start | bytes 4718596
  14.5 28.4 %all-to-all-start = ((s32[256,1,1,8]{3,2,1,0:T(1,128)}), s32[256,1,1,8]{3,2,1,0:T(1,128)S(1)}, u32[]{:S(2)}, u32[]{:S(2)}) async-start(s32[256,1,1,8]{3,2,1,0:T(1,128)} %bitcast.3), calls=%async_computation | async-start | bytes 262144 | tf_op jit(solution)/shard_map/all_to_all | solution.py:27
  30.1 7.3 %copy-start.3 = (bf16[1024,256]{1,0:T(8,128)(2,1)S(1)}, bf16[1024,256]{1,0:T(8,128)(2,1)}, u32[]{:S(2)}) copy-start(bf16[1024,256]{1,0:T(8,128)(2,1)} %param.12) | copy-start | bytes 1572868
  30.2 7.2 %copy-start.5 = (f32[256]{0:T(256)S(1)}, f32[256]{0:T(256)}, u32[]{:S(2)}) copy-start(f32[256]{0:T(256)} %param.13) | copy-start | bytes 3076
  36.1 1.3 copy-start.6
  56.5 62.4 %all-to-all-start.1 = ((f32[256,1,1,8,256]{4,3,2,1,0:T(8,128)}), f32[256,1,1,8,256]{4,3,2,1,0:T(8,128)}, u32[]{:S(2)}, u32[]{:S(2)}) async-start(f32[256,1,1,8,256]{4,3,2,1,0:T(8,128)} %fusion.10), calls=%async_computation.1 | async-start | bytes 4194304 | tf_op jit(solution)/shard_map/all_to_all | solution.py:27
  66.5 413.5 %all-reduce.4.cloned.1.call-start = ((), (), s32[]{:S(2)}) async-start(), calls=%async_computation.3 | async-start | bytes 8388608 | tf_op jit(solution)/shard_map/psum | solution.py:99
  205.4 3.8 copy-start.1
  205.4 3.8 copy-start.4
  205.4 3.8 copy-start.7
  480.0 3.6 copy-start.2
Sparse Core Ops, SparseCore 0:
  216.1 263.8 all-reduce.3
where the time goes:
time: 493 us; the launch traced here: 491 us
  waiting for transfers between devices  243 us (49%)
  blocking collectives  135 us (27%)
  other arithmetic  31.3 us (6%)
  starting transfers between devices  25.7 us (5%)
  local copies, waits for them, and re-layouts  25.3 us (5%)
  matrix products  17.1 us (3%)
  between operations  14.2 us (3%)
    psum x1, waiting for transfers between devices, per_device(): lax.psum((gw_in, gb_in, gw_out, gb_out), ('code', 'dp'))  186 us
    psum x1, blocking collectives, per_device(): lax.psum((gw_in, gb_in, gw_out, gb_out), ('code', 'dp'))  74.2 us
    all_to_all x1, blocking collectives, exchange_both(): tiles = lax.all_to_all(tiles, axis, split_axis=0, concat_axis=0, tiled=True)  60.8 us
    all_to_all x2, waiting for transfers between devices, exchange_both(): tiles = lax.all_to_all(tiles, axis, split_axis=0, concat_axis=0, tiled=True)  57.1 us
    all_to_all x2, starting transfers between devices, exchange_both(): tiles = lax.all_to_all(tiles, axis, split_axis=0, concat_axis=0, tiled=True)  25.6 us
    scatter-add x1, other arithmetic, per_device(): jax.ops.segment_sum(incoming.reshape(devices * capacity, width), row_ids,...  13.1 us
  transfers between devices with their start and end apart: 3, of which 3 were waited for; matrix products, arithmetic and copies ran while one was open for 2% of the time, Pallas kernels for 0%

commit v1 on v0

--- a/solution.py
+++ b/solution.py
@@ -1,10 +1,287 @@
 import jax
 import jax.numpy as jnp
 from jax import lax
+from jax.experimental import pallas as pl
+from jax.experimental.pallas import tpu as pltpu
 from jax.sharding import PartitionSpec as P
 
 scale_gelu = 0.7978845608028654
 cubic_term = 0.044715
+
+MESH = pl.DeviceIdType.MESH
+NX, NY, NZ = 4, 4, 8
+F32, BF16 = jnp.float32, jnp.bfloat16
+
+
+def rows(start, size):
+    return pl.ds(pl.multiple_of(start, 8), size)
+
+
+class Wires:
+    def __init__(self, send, recv):
+        self.send, self.recv, self.used, self.open = send, recv, 0, []
+
+    def start(self, src, dst, to):
+        k = self.used
+        self.used += 1
+        copy = pltpu.make_async_remote_copy(
+            src_ref=src,
+            dst_ref=dst,
+            send_sem=self.send.at[k],
+            recv_sem=self.recv.at[k],
+            device_id=to,
+            device_id_type=MESH,
+        )
+        copy.start()
+        self.open.append(copy)
+        return copy
+
+    def drain(self):
+        for copy in self.open:
+            copy.wait_send()
+
+
+AR_WIRES = 2 * (4 + 6 + 6 + 7 + 7 + 6 + 6 + 5) + 14
+
+
+def position():
+    code, dp = lax.axis_index("code"), lax.axis_index("dp")
+    return lax.div(dp, 2), lax.div(code, NZ), lax.rem(code, NZ), lax.rem(dp, 2)
+
+
+def device(x, y, z, c):
+    return (y * NZ + z, x * 2 + c)
+
+
+def ring_peers():
+    x, y, z, c = position()
+    peers = [device(x, y, z, 1 - c)]
+    peers += [device(lax.rem(x + r, NX), y, z, c) for r in range(1, NX)]
+    peers += [device(x, lax.rem(y + r, NY), z, c) for r in range(1, NY)]
+    peers += [device(x, y, lax.rem(z + r, NZ), c) for r in range(1, NZ)]
+    return peers
+
+
+class Ring:
+    def __init__(self, wires, spot, right, left, size):
+        self.w, self.p, self.n = wires, spot, size
+        self.right, self.left = right, left
+        self.h = size // 2
+
+    def chunk(self, step):
+        return lax.rem(self.p + step, 4) * self.n
+
+    def scatter_start(self, acc, base, mid, edge):
+        n, h, w = self.n, self.h, self.w
+        self.acc, self.base, self.mid, self.edge = acc, base, mid, edge
+        far, nxt, prv = (base + self.chunk(s) for s in (2, 1, 3))
+        self.nxt, self.prv = nxt, prv
+        self.far_a = w.start(acc.at[rows(far, h)], mid.at[0], self.right)
+        self.far_b = w.start(acc.at[rows(far + h, h)], mid.at[1], self.left)
+        self.near_b = w.start(acc.at[rows(nxt + h, h)], edge.at[0, pl.ds(h, h)], self.right)
+        self.near_a = w.start(acc.at[rows(prv, h)], edge.at[1, pl.ds(0, h)], self.left)
+
+    def scatter_mid(self):
+        h, w, acc = self.h, self.w, self.acc
+        self.far_a.wait_recv()
+        here = rows(self.nxt, h)
+        acc[here, :] = acc[here, :] + self.mid[0]
+        self.pass_a = w.start(acc.at[here], self.edge.at[0, pl.ds(0, h)], self.right)
+        self.far_b.wait_recv()
+        here = rows(self.prv + h, h)
+        acc[here, :] = acc[here, :] + self.mid[1]
+        self.pass_b = w.start(acc.at[here], self.edge.at[1, pl.ds(h, h)], self.left)
+
+    def scatter_end(self):
+        for copy in (self.near_b, self.near_a, self.pass_a, self.pass_b):
+            copy.wait_recv()
+        mine = self.base + self.chunk(0)
+        here = rows(mine, self.n)
+        self.acc[here, :] = self.acc[here, :] + (self.edge[0] + self.edge[1])
+        return mine
+
+    def gather_start(self, out, base, cols):
+        h, w = self.h, self.w
+        self.out, self.base, self.cols = out, base, cols
+        mine = base + self.chunk(0)
+        first, second = (out.at[rows(mine + s, h), cols] for s in (0, h))
+        self.right_a = w.start(first, first, self.right)
+        self.left_b = w.start(second, second, self.left)
+        self.right_b = w.start(second, second, self.right)
+        self.left_a = w.start(first, first, self.left)
+
+    def gather_mid(self):
+        h, w, out = self.h, self.w, self.out
+        self.right_a.wait_recv()
+        part = out.at[rows(self.base + self.chunk(3), h), self.cols]
+        self.on_a = w.start(part, part, self.right)
+        self.left_b.wait_recv()
+        part = out.at[rows(self.base + self.chunk(1) + h, h), self.cols]
+        self.on_b = w.start(part, part, self.left)
+
+    def gather_near(self):
+        self.right_b.wait_recv()
+        self.left_a.wait_recv()
+
+    def gather_far(self):
+        self.on_a.wait_recv()
+        self.on_b.wait_recv()
+
+
+def reduce_all(wires, grads, bias, out, bias_out, bufs):
+    (acc, half, mid1, edge1, mid2, edge2, deep, side0, side1, side2, side3) = bufs
+    x, y, z, c = position()
+    other = device(x, y, z, 1 - c)
+    x_right, x_left = (device(lax.rem(x + s, NX), y, z, c) for s in (1, 3))
+    y_right, y_left = (device(x, lax.rem(y + s, NY), z, c) for s in (1, 3))
+    along_x, along_y = (x, x_right, x_left), (y, y_right, y_left)
+    outer = [Ring(wires, *along_x, 256), Ring(wires, *along_y, 256)]
+    inner = [Ring(wires, *along_y, 64), Ring(wires, *along_x, 64)]
+    cols = [pl.ds(pl.multiple_of((2 * c + q) * 256, 256), 256) for q in range(2)]
+    away = [pl.ds(pl.multiple_of((2 - 2 * c + q) * 256, 256), 256) for q in range(2)]
+    order = (2, 1, 3, 0)
+
+    swaps = []
+    for step in order:
+        for q in range(2):
+            here = rows(outer[q].chunk(step), 256)
+            swaps.append(wires.start(grads.at[here, away[q]], half.at[q, here], other))
+    side = wires.start(bias, side0, other)
+    for i, step in enumerate(order):
+        for q in range(2):
+            here = rows(outer[q].chunk(step), 256)
+            swaps[2 * i + q].wait_recv()
+            acc[q, here, :] = grads[here, cols[q]] + half[q, here, :]
+    for q in range(2):
+        outer[q].scatter_start(acc.at[q], 0, mid1.at[q], edge1.at[q])
+    side.wait_recv()
+    side1[x] = bias[...] + side0[...]
+    sides = [
+        wires.start(side1.at[x], side1.at[x], device(lax.rem(x + r, NX), y, z, c))
+        for r in range(1, NX)
+    ]
+    for q in range(2):
+        outer[q].scatter_mid()
+    first = [outer[q].scatter_end() for q in range(2)]
+    for q in range(2):
+        inner[q].scatter_start(acc.at[q], first[q], mid2.at[q], edge2.at[q])
+    for copy in sides:
+        copy.wait_recv()
+    side2[y] = (side1[0] + side1[1]) + (side1[2] + side1[3])
+    sides = [
+        wires.start(side2.at[y], side2.at[y], device(x, lax.rem(y + r, NY), z, c))
+        for r in range(1, NY)
+    ]
+    for q in range(2):
+        inner[q].scatter_mid()
+    second = [inner[q].scatter_end() for q in range(2)]
+    columns = [device(x, y, lax.rem(z + r, NZ), c) for r in range(1, NZ)]
+    downs = []
+    for r in range(1, NZ):
+        for q in range(2):
+            part = acc.at[q, rows(second[q] + lax.rem(z + r, NZ) * 8, 8)]
+            downs.append(wires.start(part, deep.at[q, r - 1], columns[r - 1]))
+    for copy in sides:
+        copy.wait_recv()
+    side3[z] = (side2[0] + side2[1]) + (side2[2] + side2[3])
+    sides = [wires.start(side3.at[z], side3.at[z], to) for to in columns]
+    for copy in downs:
+        copy.wait_recv()
+    ups = []
+    for q in range(2):
+        here = rows(second[q] + z * 8, 8)
+        total = acc[q, here, :]
+        for r in range(NZ - 1):
+            total = total + deep[q, r]
+        out[here, cols[q]] = total
+        part = out.at[here, cols[q]]
+        ups += [wires.start(part, part, to) for to in columns]
+    for copy in sides:
+        copy.wait_recv()
+    total = side3[0]
+    for r in range(1, NZ):
+        total = total + side3[r]
+    bias_out[...] = total
+    for copy in ups:
+        copy.wait_recv()
+    for q in range(2):
+        inner[q].gather_start(out, first[q], cols[q])
+    for q in range(2):
+        inner[q].gather_mid()
+    for q in range(2):
+        inner[q].gather_near()
+        inner[q].gather_far()
+    for q in range(2):
+        outer[q].gather_start(out, 0, cols[q])
+    backs = []
+
+    def back(q, start, size):
+        part = out.at[rows(start, size), cols[q]]
+        backs.append(wires.start(part, part, other))
+
+    for q in range(2):
+        back(q, outer[q].chunk(0), 256)
+    for q in range(2):
+        outer[q].gather_mid()
+    for q in range(2):
+        outer[q].gather_near()
+        back(q, outer[q].chunk(3), 256)
+        back(q, outer[q].chunk(1), 256)
+    for q in range(2):
+        outer[q].on_a.wait_recv()
+        back(q, outer[q].chunk(2), 128)
+        outer[q].on_b.wait_recv()
+        back(q, outer[q].chunk(2) + 128, 128)
+    for copy in backs:
+        copy.wait_recv()
+
+
+AR_BUFS = [
+    pltpu.VMEM((2, 1024, 256), F32),
+    pltpu.VMEM((2, 1024, 256), F32),
+    pltpu.VMEM((2, 2, 128, 256), F32),
+    pltpu.VMEM((2, 2, 256, 256), F32),
+    pltpu.VMEM((2, 2, 32, 256), F32),
+    pltpu.VMEM((2, 2, 64, 256), F32),
+    pltpu.VMEM((2, 7, 8, 256), F32),
+    pltpu.VMEM((8, 256), F32),
+    pltpu.VMEM((4, 8, 256), F32),
+    pltpu.VMEM((4, 8, 256), F32),
+    pltpu.VMEM((8, 8, 256), F32),
+]
+
+
+def meet(peers):
+    barrier = pltpu.get_barrier_semaphore()
+    for peer in peers:
+        pl.semaphore_signal(barrier, inc=1, device_id=peer, device_id_type=MESH)
+    pl.semaphore_wait(barrier, len(peers))
+
+
+def reduce_kernel(grads, bias, out, bias_out, *scratch):
+    meet(ring_peers())
+    wires = Wires(scratch[-2], scratch[-1])
+    reduce_all(wires, grads, bias, out, bias_out, scratch[:-2])
+    wires.drain()
+    assert wires.used == AR_WIRES, wires.used
+
+
+def reduce_grads(grads, bias):
+    vmem = pl.BlockSpec(memory_space=pltpu.VMEM)
+    return pl.pallas_call(
+        reduce_kernel,
+        out_shape=(
+            jax.ShapeDtypeStruct((1024, 1024), F32),
+            jax.ShapeDtypeStruct((8, 256), F32),
+        ),
+        in_specs=[vmem, vmem],
+        out_specs=(vmem, vmem),
+        scratch_shapes=AR_BUFS
+        + [pltpu.SemaphoreType.DMA((AR_WIRES,)), pltpu.SemaphoreType.DMA((AR_WIRES,))],
+        compiler_params=pltpu.CompilerParams(
+            collective_id=1, has_side_effects=True, vmem_limit_bytes=60 * 2**20
+        ),
+    )(grads, bias)
 
 
 def in_blocks(array, dim, size):
@@ -64,14 +341,8 @@
     )
     valid = wanted >= 0
     row_ids = jnp.maximum(wanted, 0).reshape(-1)
-    picked = jnp.take(projected, row_ids, axis=0).reshape(n_code, n_data, capacity, width)
-    picked = jnp.where(valid[..., None], picked, 0.0)
-    answers = exchange_both(picked, ("code", "dp"), ("code", "dp"), (0, 1), (0, 1))
-    chosen = jnp.take(answers.reshape(devices * capacity, width), slots, axis=0)
-    residual = chosen - latents
-    latent_grad = cotangent - 0.25 * residual
     outgoing = (
-        jnp.zeros((devices * capacity, width), jnp.float32).at[slots].set(cotangent + residual)
+        jnp.zeros((devices * capacity, width), jnp.float32).at[slots].set(cotangent - latents)
     )
     incoming = exchange_both(
         outgoing.reshape(n_code, n_data, capacity, width),
@@ -80,8 +351,15 @@
         (0, 1),
         (0, 1),
     )
+    picked = jnp.take(projected, row_ids, axis=0).reshape(n_code, n_data, capacity, width)
+    picked = jnp.where(valid[..., None], picked, 0.0)
+    answers = exchange_both(picked, ("code", "dp"), ("code", "dp"), (0, 1), (0, 1))
+    chosen = jnp.take(answers.reshape(devices * capacity, width), slots, axis=0)
+    latent_grad = cotangent - 0.25 * (chosen - latents)
     code_grad = jax.ops.segment_sum(
-        incoming.reshape(devices * capacity, width), row_ids, num_segments=projected.shape[0]
+        (incoming + picked).reshape(devices * capacity, width),
+        row_ids,
+        num_segments=projected.shape[0],
     )
     code_low = code_grad.astype(jnp.bfloat16)
     gw_out = lax.dot_general(
@@ -96,8 +374,15 @@
         codebook, preact_grad, (((0,), (0,)), ((), ())), preferred_element_type=jnp.float32
     )
     gb_out = jnp.sum(code_grad, axis=0)
-    gw_in, gb_in, gw_out, gb_out = lax.psum((gw_in, gb_in, gw_out, gb_out), ("code", "dp"))
-    return (latent_grad, gw_in, gb_in, gw_out, gb_out)
+    wide = gw_out.reshape(4, 256, 256).transpose(1, 0, 2).reshape(256, 1024)
+    grads = jnp.concatenate([gw_in, wide], axis=0)
+    bias = jnp.concatenate(
+        [gb_in.reshape(4, 256), gb_out[None], jnp.zeros((3, 256), jnp.float32)], axis=0
+    )
+    grads, bias = reduce_grads(grads, bias)
+    gw_in = grads[:768]
+    gw_out = grads[768:].reshape(256, 4, 256).transpose(1, 0, 2).reshape(1024, 256)
+    return (latent_grad, gw_in, bias[:4].reshape(1024), gw_out, bias[4])
 
 
 def solution(mesh):

time: 493 us -> 224 us (0.45)
  waiting for transfers between devices: 243 us -> 37.3 us
  blocking collectives: 135 us -> 0 us
  Pallas kernels: 0 us -> 68.1 us
  between operations: 14.2 us -> 0.84 us
  local copies, waits for them, and re-layouts: 25.3 us -> 34.5 us
  starting transfers between devices: 25.7 us -> 32.2 us
    psum x1 -> x0, waiting for transfers between devices: 186 us -> none  [per_device(): lax.psum((gw_in, gb_in, gw_out, gb_out), ('code', 'dp'))]
    psum x1 -> x0, blocking collectives: 74.2 us -> none  [per_device(): lax.psum((gw_in, gb_in, gw_out, gb_out), ('code', 'dp'))]
    pallas_call x0 -> x1, Pallas kernels: none -> 68.1 us  [reduce_grads(): pl.pallas_call(reduce_kernel, out_shape=(jax.ShapeDtypeStruct((1024, 1024...]
    all_to_all x1 -> x0, blocking collectives: 60.8 us -> none  [exchange_both(): tiles = lax.all_to_all(tiles, axis, split_axis=0, concat_axis=0, tiled=True)]
    all_to_all x2 -> x3, waiting for transfers between devices: 57.1 us -> 37.3 us  [exchange_both(): tiles = lax.all_to_all(tiles, axis, split_axis=0, concat_axis=0, tiled=True)]
    all_to_all x2 -> x3, starting transfers between devices: 25.6 us -> 32.2 us  [exchange_both(): tiles = lax.all_to_all(tiles, axis, split_axis=0, concat_axis=0, tiled=True)]
    slice x0 -> x3, local copies, waits for them, and re-layouts: none -> 5.83 us  [the longest x1 3.97 us: per_device(): gw_in = grads[:768]]
  transfers between devices with their start and end apart: 3 -> 3, of which waited for: 3 -> 2; matrix products, arithmetic and copies ran while one was open for 2% -> 30% of each run, Pallas kernels for 0% -> 31%
where the time goes in v1:
time: 224 us; the launch traced here: 223 us
  Pallas kernels  68.1 us (30%)
  waiting for transfers between devices  37.3 us (17%)
  local copies, waits for them, and re-layouts  34.5 us (15%)
  other arithmetic  33.2 us (15%)
  starting transfers between devices  32.2 us (14%)
  matrix products  16.7 us (7%)
    pallas_call x1, Pallas kernels, reduce_grads(): pl.pallas_call(reduce_kernel, out_shape=(jax.ShapeDtypeStruct((1024, 1024...  68.1 us
    all_to_all x3, waiting for transfers between devices, exchange_both(): tiles = lax.all_to_all(tiles, axis, split_axis=0, concat_axis=0, tiled=True)  37.3 us
    all_to_all x3, starting transfers between devices, exchange_both(): tiles = lax.all_to_all(tiles, axis, split_axis=0, concat_axis=0, tiled=True)  32.2 us
    scatter-add x1, other arithmetic, per_device(): jax.ops.segment_sum((incoming + picked).reshape(devices * capacity, width...  13.8 us
    gather x1, local copies, waits for them, and re-layouts, per_device(): jnp.take(projected, row_ids, axis=0)  8.61 us
    scatter x1, other arithmetic, per_device(): jnp.zeros((devices * capacity, width), jnp.float32).at[slots]  6.94 us
    gather x1, local copies, waits for them, and re-layouts, per_device(): chosen = jnp.take(answers.reshape(devices * capacity, width), slots, axis=0)  6.35 us
    dot_general x1, matrix products, per_device(): jnp.dot(codebook, weight_in, preferred_element_type=jnp.float32) + bias_in  5.92 us
  transfers between devices with their start and end apart: 3, of which 2 were waited for; matrix products, arithmetic and copies ran while one was open for 30% of the time, Pallas kernels for 31%

profile of v1, /device:TPU:1, one launch (start us, length us, event | category | flops | bytes accessed | tf_op | source)
XLA Modules:
  0.0 222.9 jit_solution(9605795174109309362)
XLA Ops:
  0.6 1.3 convert_reduce_fusion.1
  2.0 0.7 and_reduce_fusion
  2.7 4.5 %scatter_custom_fusion = s32[2048]{0:T(1024)S(1)} fusion(s32[1024]{0:T(1024)S(1)} %bitcast.103, s32[1024]{0:T(1024)} %param.17, s32[]{:T(128)} %constant.19.clone.1), kind=kCustom, calls=%fused_computation.48 | custom fusion | bytes 8704 | tf_op jit(solution)/shard_map/scatter | solution.py:338
  7.2 0.8 reshape_transpose_transpose_reshape_reshape_reshape.6
  8.0 15.6 %all-to-all-start = ((s32[256,1,1,8]{3,2,1,0:T(1,128)}), s32[256,1,1,8]{3,2,1,0:T(1,128)S(1)}, u32[]{:S(2)}, u32[]{:S(2)}) async-start(s32[256,1,1,8]{3,2,1,0:T(1,128)} %bitcast.3), calls=%async_computation | async-start | bytes 262144 | tf_op jit(solution)/shard_map/all_to_all | solution.py:304
  23.6 6.9 %scatter_custom_fusion.1 = f32[2048,256]{1,0:T(8,128)} fusion(s32[1024]{0:T(1024)S(1)} %bitcast.104, f32[1024,256]{1,0:T(8,128)} %param.15, f32[1024,256]{1,0:T(8,128)} %param.14, f32[]{:T(128)} %constant.32.clone.1), kind=kCustom, calls=%fused_computation.29 | custom fusion | flops 262144 | bytes 4194308 | tf_op jit(solution)/shard_map/scatter | solution.py:345
  30.5 5.8 %all-to-all-done = s32[256,1,1,8]{3,2,1,0:T(1,128)S(1)} async-done(((s32[256,1,1,8]{3,2,1,0:T(1,128)}), s32[256,1,1,8]{3,2,1,0:T(1,128)S(1)}, u32[]{:S(2)}, u32[]{:S(2)}) %all-to-all-start) | async-done | bytes 8224 | tf_op jit(solution)/shard_map/all_to_all | solution.py:304
  36.3 8.9 %all-to-all-start.2 = ((f32[256,1,1,8,256]{4,3,2,1,0:T(8,128)}), f32[256,1,1,8,256]{4,3,2,1,0:T(8,128)}, u32[]{:S(2)}, u32[]{:S(2)}) async-start(f32[256,1,1,8,256]{4,3,2,1,0:T(8,128)} %bitcast.92), calls=%async_computation.2 | async-start | bytes 4194304 | tf_op jit(solution)/shard_map/all_to_all | solution.py:304
  45.3 5.9 %multiply_convert_fusion = (bf16[1024,1024]{1,0:T(8,128)(2,1)S(1)}, f32[1024,1024]{1,0:T(8,128)}) fusion(f32[1024]{0:T(1024)S(1)} %copy-done.5, bf16[1024,768]{1,0:T(8,128)(2,1)S(1)} %copy-done, bf16[768,1024]{1,0:T(8,128)(2,1)} %param.10), kind=kOutput, calls=%fused_computation.16 | convolution fusion | flops 1621098496 | bytes 9441280 | tf_op jit(solution)/shard_map/dot_general | solution.py:324
  51.2 0.7 convolution_add_fusion
  52.0 0.6 copy-done.7
  53.4 8.6 %gather_fusion = f32[2048,256]{1,0:T(8,128)} fusion(f32[1024,256]{1,0:T(8,128)S(1)} %convolution_add_fusion, s32[2048]{0:T(1024)S(1)} %broadcast_clamp_fusion), kind=kCustom, calls=%fused_computation | custom fusion | bytes 4202496 | tf_op jit(solution)/shard_map/jit(_take)/gather | solution.py:354
  62.0 4.2 %fusion.9 = f32[256,1,1,8,256]{4,3,2,1,0:T(8,128)} fusion(f32[2048,256]{1,0:T(8,128)} %gather_fusion, pred[256,8]{1,0:T(8,128)(4,1)S(1)} %fusion.34, pred[256,8]{1,0:T(8,128)(4,1)S(1)} %bitcast.101), kind=kLoop, calls=%fused_computation.23 | loop fusion | flops 1048576 | bytes 4198400 | tf_op jit(solution)/shard_map/jit(_where)/select_n | solution.py:355
  66.2 31.5 %all-to-all-done.2 = f32[256,1,1,8,256]{4,3,2,1,0:T(8,128)} async-done(((f32[256,1,1,8,256]{4,3,2,1,0:T(8,128)}), f32[256,1,1,8,256]{4,3,2,1,0:T(8,128)}, u32[]{:S(2)}, u32[]{:S(2)}) %all-to-all-start.2) | async-done | bytes 2097184 | tf_op jit(solution)/shard_map/all_to_all | solution.py:304
  97.7 7.7 %all-to-all-start.1 = ((f32[256,1,1,8,256]{4,3,2,1,0:T(8,128)}), f32[256,1,1,8,256]{4,3,2,1,0:T(8,128)}, u32[]{:S(2)}, u32[]{:S(2)}) async-start(f32[256,1,1,8,256]{4,3,2,1,0:T(8,128)} %fusion.9), calls=%async_computation.1 | async-start | bytes 4194304 | tf_op jit(solution)/shard_map/all_to_all | solution.py:304
  105.7 13.8 %scatter_custom_fusion.2 = f32[1024,256]{1,0:T(8,128)S(1)} fusion(s32[2048]{0:T(1024)S(1)} %reshape.158, f32[256,1,1,8,256]{4,3,2,1,0:T(8,128)} %all-to-all-done.2, f32[2048,256]{1,0:T(8,128)} %gather_fusion, f32[]{:T(128)} %constant.31.clone.1, f32[]{:T(128)} %constant.32.clone.1, pred[2048]{0:T(1024)(128)(4,1)S(1)} %le.43, pred[2048]{0:T(1024)(128)(4,1)S(1)} %ge.47), kind=kCustom, calls=%fused_computation.21 | custom fusion | flops 2097152 | bytes 5248512 | tf_op jit(solution)/shard_map/scatter-add | solution.py:359
  119.7 2.3 %fusion.20 = f32[1024,256]{1,0:T(8,128)S(1)} fusion(bf16[1024,1024]{1,0:T(8,128)(2,1)} %copy-done.7, f32[1024,256]{1,0:T(8,128)S(1)} %scatter_custom_fusion.2), kind=kOutput, calls=%fused_computation.37 | convolution fusion | flops 537133056 | bytes 4194304 | tf_op jit(solution)/shard_map/dot_general | solution.py:365
  122.1 0.7 copy.45
  122.8 1.2 copy.48
  123.9 0.7 copy-done.8
  124.6 4.2 %convert_reduce_fusion = (f32[1024]{0:T(1024)S(1)}, bf16[1024,1024]{1,0:T(8,128)(2,1)}) fusion(f32[1024,1024]{1,0:T(8,128)S(1)} %copy-done.8, f32[1024]{0:T(1024)S(1)} %copy-done.5, bf16[1024,256]{1,0:T(8,128)(2,1)S(1)} %copy-done.4, f32[1024,256]{1,0:T(8,128)S(1)} %scatter_custom_fusion.2), kind=kOutput, calls=%fused_computation.15 | convolution fusion | flops 560200704 | bytes 7872512 | tf_op jit(solution)/shard_map/dot_general | solution.py:368
  128.8 3.6 %convolution_bitcast_fusion = f32[768,1024]{1,0:T(8,128)S(1)} fusion(bf16[1024,1024]{1,0:T(8,128)(2,1)} %get-tuple-element.14, bf16[1024,768]{1,0:T(8,128)(2,1)S(1)} %copy-done), kind=kOutput, calls=%fused_computation.26 | convolution fusion | flops 1610612736 | bytes 6815744 | tf_op jit(solution)/shard_map/dot_general | solution.py:373
  132.4 2.2 %pad_maximum_fusion.grads = f32[1024,1024]{1,0:T(8,128)} fusion(f32[256,1024]{1,0:T(8,128)S(1)} %bitcast.95, f32[768,1024]{1,0:T(8,128)S(1)} %convolution_bitcast_fusion), kind=kLoop, calls=%fused_computation.14 | loop fusion | flops 1048576 | bytes 8388608 | tf_op jit(solution)/shard_map/concatenate | solution.py:378
  134.6 0.7 maximum_maximum_fusion.bias
  135.3 68.1 %shard_map.128 = (f32[1024,1024]{1,0:T(8,128)}, f32[8,256]{1,0:T(8,128)}) custom-call(f32[1024,1024]{1,0:T(8,128)} %pad_maximum_fusion.grads, f32[8,256]{1,0:T(8,128)} %maximum_maximum_fusion.bias), custom_call_target="tpu_custom_call" | custom-call | tf_op jit(solution)/shard_map/pallas_call | solution.py:271
  203.5 1.3 slice.14
  204.8 4.0 %slice.12 = f32[768,1024]{1,0:T(8,128)} slice(f32[1024,1024]{1,0:T(8,128)} %get-tuple-element.7), slice={[0:768], [0:1024]} | slice | bytes 6291456 | tf_op jit(solution)/shard_map/slice | solution.py:383
  209.3 0.6 copy.49
  209.9 1.4 reshape.150
  211.4 2.4 %copy.46 = f32[4,256,256]{2,1,0:T(8,128)} copy(f32[4,256,256]{2,0,1:T(4,128)} %bitcast.94) | data formatting | bytes 2097152 | tf_op jit(solution)/shard_map/transpose | solution.py:384
  213.8 6.4 %gather_fusion.1 = f32[1024,256]{1,0:T(8,128)} fusion(f32[2048,256]{1,0:T(8,128)} %bitcast.22, s32[1024]{0:T(1024)S(1)} %broadcast_clamp_fusion.1), kind=kCustom, calls=%fused_computation.1 | custom fusion | bytes 2101248 | tf_op jit(solution)/shard_map/jit(_take)/gather | solution.py:357
  220.1 2.7 %multiply_subtract_fusion = f32[1024,256]{1,0:T(8,128)} fusion(f32[1024,256]{1,0:T(8,128)S(1)} %copy-done.1, f32[1024,256]{1,0:T(8,128)} %param.14, f32[1024,256]{1,0:T(8,128)} %gather_fusion.1, pred[1024]{0:T(1024)(128)(4,1)S(1)} %get-tuple-element.9), kind=kLoop, calls=%fused_computation.33 | loop fusion | flops 1048576 | bytes 4195328 | tf_op jit(solution)/shard_map/sub | solution.py:358
  (35 shorter events, 1.9 us)
Async XLA Ops:
  0.6 44.6 %copy-start = (bf16[1024,768]{1,0:T(8,128)(2,1)S(1)}, bf16[1024,768]{1,0:T(8,128)(2,1)}, u32[]{:S(2)}) copy-start(bf16[1024,768]{1,0:T(8,128)(2,1)} %param.9) | copy-start | bytes 4718596
  8.0 28.4 %all-to-all-start = ((s32[256,1,1,8]{3,2,1,0:T(1,128)}), s32[256,1,1,8]{3,2,1,0:T(1,128)S(1)}, u32[]{:S(2)}, u32[]{:S(2)}) async-start(s32[256,1,1,8]{3,2,1,0:T(1,128)} %bitcast.3), calls=%async_computation | async-start | bytes 262144 | tf_op jit(solution)/shard_map/all_to_all | solution.py:304
  30.5 14.7 %copy-start.5 = (f32[1024]{0:T(1024)S(1)}, f32[1024]{0:T(1024)}, u32[]{:S(2)}) copy-start(f32[1024]{0:T(1024)} %param.11) | copy-start | bytes 12292
  36.3 61.4 %all-to-all-start.2 = ((f32[256,1,1,8,256]{4,3,2,1,0:T(8,128)}), f32[256,1,1,8,256]{4,3,2,1,0:T(8,128)}, u32[]{:S(2)}, u32[]{:S(2)}) async-start(f32[256,1,1,8,256]{4,3,2,1,0:T(8,128)} %bitcast.92), calls=%async_computation.2 | async-start | bytes 4194304 | tf_op jit(solution)/shard_map/all_to_all | solution.py:304
  45.3 5.9 %copy-start.4 = (bf16[1024,256]{1,0:T(8,128)(2,1)S(1)}, bf16[1024,256]{1,0:T(8,128)(2,1)}, u32[]{:S(2)}) copy-start(bf16[1024,256]{1,0:T(8,128)(2,1)} %param.12) | copy-start | bytes 1572868
  45.3 5.9 %copy-start.6 = (f32[256]{0:T(256)S(1)}, f32[256]{0:T(256)}, u32[]{:S(2)}) copy-start(f32[256]{0:T(256)} %param.13) | copy-start | bytes 3076
  51.2 1.3 copy-start.7
  97.7 116.0 %all-to-all-start.1 = ((f32[256,1,1,8,256]{4,3,2,1,0:T(8,128)}), f32[256,1,1,8,256]{4,3,2,1,0:T(8,128)}, u32[]{:S(2)}, u32[]{:S(2)}) async-start(f32[256,1,1,8,256]{4,3,2,1,0:T(8,128)} %fusion.9), calls=%async_computation.1 | async-start | bytes 4194304 | tf_op jit(solution)/shard_map/all_to_all | solution.py:304
  122.1 2.6 %copy-start.8 = (f32[1024,1024]{1,0:T(8,128)S(1)}, f32[1024,1024]{1,0:T(8,128)}, u32[]{:S(2)}) copy-start(f32[1024,1024]{1,0:T(8,128)} %get-tuple-element.12) | copy-start | bytes 12582916
  128.8 3.6 %copy-start.2 = (f32[32,8,4,256]{3,1,2,0:T(8,128)S(1)}, f32[32,8,4,256]{3,1,2,0:T(8,128)}, u32[]{:S(2)}) copy-start(f32[32,8,4,256]{3,1,2,0:T(8,128)} %copy.48) | copy-start | bytes 3145732
  204.8 4.0 %copy-start.3 = (f32[8,256]{1,0:T(8,128)S(1)}, f32[8,256]{1,0:T(8,128)}, u32[]{:S(2)}) copy-start(f32[8,256]{1,0:T(8,128)} %get-tuple-element.8) | copy-start | bytes 24580
  213.8 6.4 %copy-start.1 = (f32[1024,256]{1,0:T(8,128)S(1)}, f32[1024,256]{1,0:T(8,128)}, u32[]{:S(2)}) copy-start(f32[1024,256]{1,0:T(8,128)} %param.15) | copy-start | bytes 3145732

commit v2 on v1

--- a/solution.py
+++ b/solution.py
@@ -10,6 +10,7 @@
 
 MESH = pl.DeviceIdType.MESH
 NX, NY, NZ = 4, 4, 8
+CAP, DEVICES = 8, 256
 F32, BF16 = jnp.float32, jnp.bfloat16
 
 
@@ -128,26 +129,42 @@
         self.on_b.wait_recv()
 
 
-def reduce_all(wires, grads, bias, out, bias_out, bufs):
-    (acc, half, mid1, edge1, mid2, edge2, deep, side0, side1, side2, side3) = bufs
+def rings(wires):
     x, y, z, c = position()
-    other = device(x, y, z, 1 - c)
     x_right, x_left = (device(lax.rem(x + s, NX), y, z, c) for s in (1, 3))
     y_right, y_left = (device(x, lax.rem(y + s, NY), z, c) for s in (1, 3))
     along_x, along_y = (x, x_right, x_left), (y, y_right, y_left)
     outer = [Ring(wires, *along_x, 256), Ring(wires, *along_y, 256)]
     inner = [Ring(wires, *along_y, 64), Ring(wires, *along_x, 64)]
-    cols = [pl.ds(pl.multiple_of((2 * c + q) * 256, 256), 256) for q in range(2)]
+    return outer, inner
+
+
+ORDER = (2, 1, 3, 0)
+
+
+def swap_start(wires, grads, bufs):
+    half = bufs[1]
+    x, y, z, c = position()
     away = [pl.ds(pl.multiple_of((2 - 2 * c + q) * 256, 256), 256) for q in range(2)]
-    order = (2, 1, 3, 0)
-
+    outer, _ = rings(wires)
     swaps = []
-    for step in order:
+    for step in ORDER:
         for q in range(2):
             here = rows(outer[q].chunk(step), 256)
-            swaps.append(wires.start(grads.at[here, away[q]], half.at[q, here], other))
+            swaps.append(
+                wires.start(grads.at[here, away[q]], half.at[q, here], device(x, y, z, 1 - c))
+            )
+    return swaps
+
+
+def reduce_all(wires, swaps, grads, bias, out, bias_out, bufs, between):
+    (acc, half, mid1, edge1, mid2, edge2, deep, side0, side1, side2, side3) = bufs
+    x, y, z, c = position()
+    other = device(x, y, z, 1 - c)
+    outer, inner = rings(wires)
+    cols = [pl.ds(pl.multiple_of((2 * c + q) * 256, 256), 256) for q in range(2)]
     side = wires.start(bias, side0, other)
-    for i, step in enumerate(order):
+    for i, step in enumerate(ORDER):
         for q in range(2):
             here = rows(outer[q].chunk(step), 256)
             swaps[2 * i + q].wait_recv()
@@ -227,6 +244,7 @@
         outer[q].gather_near()
         back(q, outer[q].chunk(3), 256)
         back(q, outer[q].chunk(1), 256)
+    between()
     for q in range(2):
         outer[q].on_a.wait_recv()
         back(q, outer[q].chunk(2), 128)
@@ -251,138 +269,302 @@
 ]
 
 
-def meet(peers):
+def linear(x, y, z, c):
+    return ((y * NZ + z) * NX + x) * 2 + c
+
+
+def partner(i):
+    x, y, z, c = position()
+    z = lax.rem(z + lax.rem(i, 8), NZ)
+    x = lax.rem(x + lax.rem(lax.div(i, 8), 4), NX)
+    y = lax.rem(y + lax.rem(lax.div(i, 32), 4), NY)
+    c = lax.rem(c + lax.div(i, 128), 2)
+    return device(x, y, z, c), linear(x, y, z, c)
+
+
+def greet(peers, sem):
+    for peer in peers:
+        pl.semaphore_signal(sem, inc=1, device_id=peer, device_id_type=MESH)
+
+
+def spread(source, target, send, recv):
+    me = linear(*position())
+
+    def one(i, carry):
+        to, index = partner(i)
+        pltpu.make_async_remote_copy(
+            src_ref=source.at[index],
+            dst_ref=target.at[me],
+            send_sem=send,
+            recv_sem=recv,
+            device_id=to,
+            device_id_type=MESH,
+        ).start()
+        return carry
+
+    lax.fori_loop(1, DEVICES, one, 0)
+    target[me] = source[me]
+    to, _ = partner(1)
+    return pltpu.make_async_remote_copy(
+        src_ref=source.at[pl.ds(0, DEVICES - 1)],
+        dst_ref=target.at[pl.ds(0, DEVICES - 1)],
+        send_sem=send,
+        recv_sem=recv,
+        device_id=to,
+        device_id_type=MESH,
+    )
+
+
+def dot(a, b):
+    return jnp.dot(a, b, preferred_element_type=F32)
+
+
+def halves(value):
+    high = value.astype(BF16)
+    low = (value - high.astype(F32)).astype(BF16)
+    return jnp.concatenate([high, low], axis=1)
+
+
+def joined(value):
+    return value[:, :256] + value[:, 256:]
+
+
+def upright(row):
+    return jnp.transpose(jnp.broadcast_to(row, (128, row.shape[1])))
+
+
+def iota(shape, dim):
+    return lax.broadcasted_iota(jnp.int32, shape, dim).astype(F32)
+
+
+def one_hot(condition):
+    return jnp.where(condition, 1.0, 0.0).astype(BF16)
+
+
+def whole_kernel(
+    codebook_h, weight_in_h, bias_in, weight_out_h, bias_out, latents, cotangent, owner, code,
+    latent_grad, out, side_out,
+    codebook, weight_in, weight_out, slot_col, values, send_a, recv_a, send_b, recv_b, ids_out, ids_in,
+    slope, hidden_t, codebook_t, weight_out_t, projected, base, picks, code_low, grads, side,
+    load, ids_s, ids_r, a_s, a_r, b_s, b_r, near_a, near_b, wire_s, wire_r, *bufs,
+):
+    x, y, z, c = position()
+    loads = [
+        pltpu.make_async_copy(src, dst, load.at[i])
+        for i, (src, dst) in enumerate(
+            ((codebook_h, codebook), (weight_in_h, weight_in), (weight_out_h, weight_out))
+        )
+    ]
+    for copy in loads:
+        copy.start()
     barrier = pltpu.get_barrier_semaphore()
-    for peer in peers:
-        pl.semaphore_signal(barrier, inc=1, device_id=peer, device_id_type=MESH)
-    pl.semaphore_wait(barrier, len(peers))
-
-
-def reduce_kernel(grads, bias, out, bias_out, *scratch):
-    meet(ring_peers())
-    wires = Wires(scratch[-2], scratch[-1])
-    reduce_all(wires, grads, bias, out, bias_out, scratch[:-2])
+    row_peers = [
+        device(lax.rem(x + r, NX), y, z, lax.rem(c + s, 2))
+        for r in range(NX) for s in range(2) if r + s
+    ]
+    y_peers = [device(x, lax.rem(y + r, NY), z, c) for r in range(1, NY)]
+    z_peers = [device(x, y, lax.rem(z + r, NZ), c) for r in range(1, NZ)]
+    line_peers = row_peers + y_peers + z_peers
+    greet(line_peers, barrier)
+
+    owner_row = owner[...].astype(F32)
+    code_row = code[...].astype(F32) + 1.0
+    owner_col = upright(owner_row)
+    lower = iota((128, 128), 0) < iota((128, 128), 1)
+    ranks = []
+    for i in range(8):
+        name = owner_row[:, 128 * i : 128 * i + 128]
+        count = jnp.where((owner_col[128 * i : 128 * i + 128] == name) & lower, 1.0, 0.0)
+        for j in range(i):
+            count += jnp.where(owner_col[128 * j : 128 * j + 128] == name, 1.0, 0.0)
+        ranks.append(jnp.sum(count, axis=0, keepdims=True))
+    rank_row = jnp.concatenate(ranks, axis=1)
+    slot_row = owner_row * CAP + rank_row
+    slot_col[...] = upright(slot_row)
+    pl.semaphore_wait(barrier, len(line_peers))
+    greet(row_peers, near_a)
+
+    rank_col = upright(rank_row)
+    code_col = upright(code_row)
+    code_high = jnp.floor(code_col * (1.0 / 32))
+    mine = rank_col == iota((1024, 128), 1)
+    digits = jnp.concatenate(
+        [
+            jnp.where(mine, code_high, 0.0).astype(BF16),
+            jnp.where(mine, code_col - 32.0 * code_high, 0.0).astype(BF16),
+        ],
+        axis=1,
+    )
+    named = dot(one_hot(owner_row == iota((256, 1024), 0)), digits)
+    ids_out[:, 0, :] = named[:, :128] * 32.0 + named[:, 128:] - 1.0
+    values[pl.ds(0, 1024), :] = halves(cotangent[...] - latents[...])
+    pl.semaphore_wait(near_a, len(row_peers))
+    greet(y_peers, near_b)
+
+    def arrange(i, carry):
+        hot = one_hot(slot_row == iota((256, 1024), 0) + (i * 256).astype(F32))
+        block = joined(dot(hot, values[pl.ds(0, 1024), :]))
+        send_a[pl.ds(i * 32, 32)] = block.reshape(32, CAP, 256)
+        return carry
+
+    lax.fori_loop(0, 8, arrange, 0)
+    pl.semaphore_wait(near_b, len(y_peers))
+    ids_all = spread(ids_out, ids_in, ids_s, ids_r)
+    rows_all = spread(send_a, recv_a, a_s, a_r)
+
+    for copy in loads:
+        copy.wait()
+    weight_out_t[...] = jnp.transpose(weight_out[...].astype(F32)).astype(BF16)
+
+    def forward(i, carry):
+        here = rows(i * 256, 256)
+        block = codebook[here, :]
+        pre = dot(block, weight_in[...]) + bias_in[...]
+        tangent = jnp.tanh(scale_gelu * (pre + cubic_term * pre * pre * pre))
+        value = 0.5 * pre * (1.0 + tangent)
+        slope[here, :] = 0.5 * (1.0 + tangent) + 0.5 * pre * (
+            1.0 - tangent * tangent
+        ) * scale_gelu * (1.0 + 3.0 * cubic_term * pre * pre)
+        hidden = value.astype(BF16)
+        cols = pl.ds(pl.multiple_of(i * 256, 256), 256)
+        hidden_t[:, cols] = jnp.transpose(value).astype(BF16)
+        codebook_t[:, cols] = jnp.transpose(block.astype(F32)).astype(BF16)
+        block = dot(hidden, weight_out[...]) + bias_out[...]
+        base[here, :] = block
+        projected[here, :] = halves(block)
+        return carry
+
+    lax.fori_loop(0, 4, forward, 0)
+
+    ids_all.wait_recv()
+    ids = ids_in[:, 0, :]
+    ids_t = jnp.transpose(ids)
+    ones = jnp.ones((256, 128), BF16)
+    for j in range(CAP):
+        hot = one_hot(ids[:, j : j + 1] == iota((256, 1024), 1))
+        send_b[:, j, :] = joined(dot(hot, projected[...]))
+        for i in range(4):
+            hot = one_hot(ids_t[j : j + 1, :] == iota((256, 256), 0) + 256.0 * i)
+            picks[j, pl.ds(i * 256, 256), :] = hot
+    for i in range(4):
+        here = pl.ds(i * 256, 256)
+        count = dot(picks[0, here, :], ones)
+        for j in range(1, CAP):
+            count += dot(picks[j, here, :], ones)
+        base[here, :] = base[here, :] * jnp.concatenate([count, count], axis=1)
+
+    rows_all.wait_recv()
+    back_all = spread(send_b, recv_b, b_s, b_r)
+    for j in range(CAP):
+        values[pl.ds(j * 256, 256), :] = halves(recv_a[:, j, :])
+    side_rows = []
+    for i in range(4):
+        here = pl.ds(i * 256, 256)
+        total = dot(picks[0, here, :], values[pl.ds(0, 256), :])
+        for j in range(1, CAP):
+            total += dot(picks[j, here, :], values[pl.ds(j * 256, 256), :])
+        total = base[here, :] + joined(total)
+        code_low[here, :] = total.astype(BF16)
+        side_rows.append(jnp.sum(total, axis=0, keepdims=True))
+    side[...] = jnp.zeros((8, 256), F32)
+    side[4:5, :] = (side_rows[0] + side_rows[1]) + (side_rows[2] + side_rows[3])
+
+    def gradient(b):
+        cols = pl.ds(pl.multiple_of(b * 256, 256), 256)
+        back = dot(code_low[...], weight_out_t[:, cols])
+        low = (back * slope[:, cols]).astype(BF16)
+        side[pl.ds(b, 1), :] = jnp.sum(low.astype(F32), axis=0, keepdims=True)
+        grads[pl.ds(0, 768), cols] = dot(codebook_t[...], low)
+        grads[pl.ds(768, 256), cols] = dot(hidden_t[rows(b * 256, 256), :], code_low[...])
+
+    for q in range(2):
+        gradient(2 - 2 * c + q)
+    wires = Wires(wire_s, wire_r)
+    swaps = swap_start(wires, grads, bufs)
+    for q in range(2):
+        gradient(2 * c + q)
+
+    def chosen():
+        back_all.wait_recv()
+        for j in range(8):
+            values[pl.ds(j * 256, 256), :] = halves(recv_b[pl.ds(j * 32, 32)].reshape(256, 256))
+
+        def pick(i, carry):
+            here = rows(i * 256, 256)
+            slot = slot_col[here, :]
+            total = jnp.zeros((256, 512), F32)
+            for j in range(8):
+                hot = jnp.concatenate(
+                    [one_hot(slot == iota((256, 128), 1) + float(j * 256 + k * 128)) for k in range(2)],
+                    axis=1,
+                )
+                total += dot(hot, values[pl.ds(j * 256, 256), :])
+            residual = joined(total) - latents[here, :]
+            latent_grad[here, :] = cotangent[here, :] - 0.25 * residual
+            return carry
+
+        lax.fori_loop(0, 4, pick, 0)
+
+    reduce_all(wires, swaps, grads, side, out, side_out, bufs, chosen)
     wires.drain()
+    ids_all.wait_send()
+    rows_all.wait_send()
+    back_all.wait_send()
     assert wires.used == AR_WIRES, wires.used
 
 
-def reduce_grads(grads, bias):
-    vmem = pl.BlockSpec(memory_space=pltpu.VMEM)
+def whole(codebook, weight_in, bias_in, weight_out, bias_out, latents, cotangent, owner, code):
+    vmem, anywhere = (pl.BlockSpec(memory_space=m) for m in (pltpu.VMEM, pl.ANY))
+    dma, plain = pltpu.SemaphoreType.DMA, pltpu.SemaphoreType.REGULAR
+    scratch = [
+        pltpu.VMEM((1024, 768), BF16),
+        pltpu.VMEM((768, 1024), BF16),
+        pltpu.VMEM((1024, 256), BF16),
+        pltpu.VMEM((1024, 128), F32),
+        pltpu.VMEM((2048, 512), BF16),
+    ]
+    scratch += [pltpu.VMEM((DEVICES, CAP, 256), F32)] * 4
+    scratch += [pltpu.VMEM((DEVICES, 1, 128), F32)] * 2
+    scratch += [
+        pltpu.VMEM((1024, 1024), F32),
+        pltpu.VMEM((1024, 1024), BF16),
+        pltpu.VMEM((768, 1024), BF16),
+        pltpu.VMEM((256, 1024), BF16),
+        pltpu.VMEM((1024, 512), BF16),
+        pltpu.VMEM((1024, 256), F32),
+        pltpu.VMEM((CAP, 1024, 256), BF16),
+        pltpu.VMEM((1024, 256), BF16),
+        pltpu.VMEM((1024, 1024), F32),
+        pltpu.VMEM((8, 256), F32),
+        dma((3,)), dma, dma, dma, dma, dma, dma, plain, plain,
+        dma((AR_WIRES,)), dma((AR_WIRES,)),
+    ]
     return pl.pallas_call(
-        reduce_kernel,
+        whole_kernel,
         out_shape=(
+            jax.ShapeDtypeStruct((1024, 256), F32),
             jax.ShapeDtypeStruct((1024, 1024), F32),
             jax.ShapeDtypeStruct((8, 256), F32),
         ),
-        in_specs=[vmem, vmem],
-        out_specs=(vmem, vmem),
-        scratch_shapes=AR_BUFS
-        + [pltpu.SemaphoreType.DMA((AR_WIRES,)), pltpu.SemaphoreType.DMA((AR_WIRES,))],
+        in_specs=[anywhere, anywhere, vmem, anywhere, vmem, vmem, vmem, vmem, vmem],
+        out_specs=(vmem, vmem, vmem),
+        scratch_shapes=scratch + AR_BUFS,
         compiler_params=pltpu.CompilerParams(
-            collective_id=1, has_side_effects=True, vmem_limit_bytes=60 * 2**20
+            collective_id=1, has_side_effects=True, vmem_limit_bytes=62 * 2**20
         ),
-    )(grads, bias)
-
-
-def in_blocks(array, dim, size):
-    before, after = (array.shape[:dim], array.shape[dim + 1 :])
-    return jnp.moveaxis(array.reshape(*before, size, -1, *after), dim, 0)
-
-
-def in_order(tiles, dim):
-    shape = list(tiles.shape[1:])
-    shape[dim] *= tiles.shape[0]
-    return jnp.moveaxis(tiles, 0, dim).reshape(shape)
-
-
-def exchange_both(array, axis, axes, splits, concats):
-    sizes = [lax.axis_size(a) for a in axes]
-    tiles = in_blocks(array, splits[0], sizes[0])
-    tiles = jnp.moveaxis(in_blocks(tiles, splits[1] + 1, sizes[1]), 0, 1)
-    inside = tiles.shape[2:]
-    tiles = tiles.reshape(-1, *inside)
-    tiles = lax.all_to_all(tiles, axis, split_axis=0, concat_axis=0, tiled=True)
-    tiles = in_order(tiles.reshape(*sizes, *inside), concats[0] + 1)
-    return in_order(tiles, concats[1])
-
-
-def gelu_value(x):
-    inner = scale_gelu * (x + cubic_term * x * x * x)
-    return 0.5 * x * (1.0 + jnp.tanh(inner))
-
-
-def gelu_slope(x):
-    tangent = jnp.tanh(scale_gelu * (x + cubic_term * x * x * x))
-    return 0.5 * (1.0 + tangent) + 0.5 * x * (1.0 - tangent * tangent) * scale_gelu * (
-        1.0 + 3.0 * cubic_term * x * x
-    )
+    )(codebook, weight_in, bias_in, weight_out, bias_out, latents, cotangent, owner, code)
 
 
 def per_device(
     codebook, weight_in, bias_in, weight_out, bias_out, latents, cotangent, code_owner, code_row
 ):
-    preact = jnp.dot(codebook, weight_in, preferred_element_type=jnp.float32) + bias_in
-    hidden = gelu_value(preact).astype(jnp.bfloat16)
-    projected = jnp.dot(hidden, weight_out, preferred_element_type=jnp.float32) + bias_out
-    n_code = lax.axis_size("code")
-    n_data = lax.axis_size("dp")
-    devices = n_code * n_data
-    owners = code_owner[:, 0]
-    count = owners.shape[0]
-    width = latents.shape[1]
-    capacity = max(2, 2 * count // devices)
-    position = jnp.arange(count, dtype=jnp.int32)
-    same = (owners[:, None] == owners[None, :]) & (position[None, :] < position[:, None])
-    ranks = jnp.sum(same.astype(jnp.int32), axis=1)
-    slots = owners * capacity + ranks
-    wanted = jnp.full((devices * capacity,), -1, jnp.int32).at[slots].set(code_row)
-    wanted = exchange_both(
-        wanted.reshape(n_code, n_data, capacity), ("code", "dp"), ("code", "dp"), (0, 1), (0, 1)
+    latent_grad, grads, side = whole(
+        codebook, weight_in, bias_in[None], weight_out, bias_out[None], latents, cotangent,
+        code_owner.reshape(1, 1024), code_row.reshape(1, 1024),
     )
-    valid = wanted >= 0
-    row_ids = jnp.maximum(wanted, 0).reshape(-1)
-    outgoing = (
-        jnp.zeros((devices * capacity, width), jnp.float32).at[slots].set(cotangent - latents)
-    )
-    incoming = exchange_both(
-        outgoing.reshape(n_code, n_data, capacity, width),
-        ("code", "dp"),
-        ("code", "dp"),
-        (0, 1),
-        (0, 1),
-    )
-    picked = jnp.take(projected, row_ids, axis=0).reshape(n_code, n_data, capacity, width)
-    picked = jnp.where(valid[..., None], picked, 0.0)
-    answers = exchange_both(picked, ("code", "dp"), ("code", "dp"), (0, 1), (0, 1))
-    chosen = jnp.take(answers.reshape(devices * capacity, width), slots, axis=0)
-    latent_grad = cotangent - 0.25 * (chosen - latents)
-    code_grad = jax.ops.segment_sum(
-        (incoming + picked).reshape(devices * capacity, width),
-        row_ids,
-        num_segments=projected.shape[0],
-    )
-    code_low = code_grad.astype(jnp.bfloat16)
-    gw_out = lax.dot_general(
-        hidden, code_low, (((0,), (0,)), ((), ())), preferred_element_type=jnp.float32
-    )
-    back = lax.dot_general(
-        code_low, weight_out, (((1,), (1,)), ((), ())), preferred_element_type=jnp.float32
-    )
-    preact_grad = (back * gelu_slope(preact)).astype(jnp.bfloat16)
-    gb_in = jnp.sum(preact_grad.astype(jnp.float32), axis=0)
-    gw_in = lax.dot_general(
-        codebook, preact_grad, (((0,), (0,)), ((), ())), preferred_element_type=jnp.float32
-    )
-    gb_out = jnp.sum(code_grad, axis=0)
-    wide = gw_out.reshape(4, 256, 256).transpose(1, 0, 2).reshape(256, 1024)
-    grads = jnp.concatenate([gw_in, wide], axis=0)
-    bias = jnp.concatenate(
-        [gb_in.reshape(4, 256), gb_out[None], jnp.zeros((3, 256), jnp.float32)], axis=0
-    )
-    grads, bias = reduce_grads(grads, bias)
     gw_in = grads[:768]
     gw_out = grads[768:].reshape(256, 4, 256).transpose(1, 0, 2).reshape(1024, 256)
-    return (latent_grad, gw_in, bias[:4].reshape(1024), gw_out, bias[4])
+    return (latent_grad, gw_in, side[:4].reshape(1024), gw_out, side[4])
 
 
 def solution(mesh):

time: 224 us -> 172 us (0.77)
  Pallas kernels: 68.1 us -> 161 us
  waiting for transfers between devices: 37.3 us -> 0 us
  other arithmetic: 33.2 us -> 0 us
  starting transfers between devices: 32.2 us -> 0 us
  local copies, waits for them, and re-layouts: 34.5 us -> 10.4 us
  matrix products: 16.7 us -> 0 us
    pallas_call x1, Pallas kernels: 68.1 us -> 161 us  [whole(): pl.pallas_call(whole_kernel, out_shape=(jax.ShapeDtypeStruct((1024, 256),...]
    all_to_all x3 -> x0, waiting for transfers between devices: 37.3 us -> none  [exchange_both(): tiles = lax.all_to_all(tiles, axis, split_axis=0, concat_axis=0, tiled=True)]
    all_to_all x3 -> x0, starting transfers between devices: 32.2 us -> none  [exchange_both(): tiles = lax.all_to_all(tiles, axis, split_axis=0, concat_axis=0, tiled=True)]
    dot_general x5 -> x0, matrix products: 16.7 us -> none  [the longest x1 5.92 us: per_device(): jnp.dot(codebook, weight_in, preferred_element_type=jnp.float32) + bias_in]
    gather x2 -> x0, local copies, waits for them, and re-layouts: 15 us -> none  [the longest x1 8.61 us: per_device(): jnp.take(projected, row_ids, axis=0)]
    scatter-add x1 -> x0, other arithmetic: 13.8 us -> none  [per_device(): jax.ops.segment_sum((incoming + picked).reshape(devices * capacity, width...]
    scatter x1 -> x0, other arithmetic: 6.94 us -> none  [per_device(): jnp.zeros((devices * capacity, width), jnp.float32).at[slots]]
    scatter x1 -> x0, local copies, waits for them, and re-layouts: 4.47 us -> none  [per_device(): jnp.full((devices * capacity,), -1, jnp.int32).at[slots].set(code_row)]
  transfers between devices with their start and end apart: 3 -> 0, of which waited for: 2 -> 0; matrix products, arithmetic and copies ran while one was open for 30% -> 0% of each run, Pallas kernels for 31% -> 0%
where the time goes in v2:
time: 172 us
  Pallas kernels  161 us (94%)
  local copies, waits for them, and re-layouts  10.4 us (6%)
    pallas_call x1, Pallas kernels, whole(): pl.pallas_call(whole_kernel, out_shape=(jax.ShapeDtypeStruct((1024, 256),...  161 us
    slice x1, local copies, waits for them, and re-layouts, per_device(): gw_in = grads[:768]  3.97 us

profile of v2, /device:TPU:1, one launch (start us, length us, event | category | flops | bytes accessed | tf_op | source)
XLA Modules:
  0.0 171.6 jit_solution(11009308636727866039)
XLA Ops:
  0.6 160.5 %shard_map.128 = (f32[1024,256]{1,0:T(8,128)}, f32[1024,1024]{1,0:T(8,128)}, f32[8,256]{1,0:T(8,128)}) custom-call(bf16[1024,768]{1,0:T(8,128)(2,1)} %codebook_h.1, bf16[768,1024]{1,0:T(8,128)(2,1)} %weight_in_h.1, f32[1,1024]{1,0:T(1,128)} %bitcast.13, bf16[1024,256]{1,0:T(8,128)(2,1)} %weight_out_h.1, f32[1,256]{1,0:T(1,128)} %bitcast.17, ...), custom_call_target="tpu_custom_call" | custom-call | tf_op jit(solution)/shard_map/pallas_call | solution.py:542
  161.2 1.3 slice.15
  162.4 0.7 slice_bitcast_fusion
  163.1 0.6 copy.15
  163.7 1.3 slice.14
  165.0 4.0 %slice.12 = f32[768,1024]{1,0:T(8,128)} slice(f32[1024,1024]{1,0:T(8,128)} %get-tuple-element.9), slice={[0:768], [0:1024]} | slice | bytes 6291456 | tf_op jit(solution)/shard_map/slice | solution.py:565
  169.0 0.0 copy-start
  169.0 0.5 reshape.28
  169.5 1.2 copy.14
  170.7 0.0 copy-done
  170.7 1.0 copy.17
Async XLA Ops:
  169.0 1.7 copy-start

commit v3 on v2

v3 whole, which is shorter than its diff:
```python
import jax
import jax.numpy as jnp
from jax import lax
from jax.experimental import pallas as pl
from jax.experimental.pallas import tpu as pltpu
from jax.sharding import PartitionSpec as P

scale_gelu = 0.7978845608028654
cubic_term = 0.044715


MESH = pl.DeviceIdType.MESH
NX, NY, NZ = 4, 4, 8
CAP, DEVICES, GROUPS, CODES = 8, 256, 8, 32
PACE = 4
LANES = 128
F32, BF16 = jnp.float32, jnp.bfloat16


def rows(start, size):
    return pl.ds(pl.multiple_of(start, 8), size)


class Wires:
    def __init__(self, send, recv):
        self.send, self.recv, self.used, self.open = send, recv, 0, []

    def start(self, src, dst, to):
        k = self.used
        self.used += 1
        copy = pltpu.make_async_remote_copy(
            src_ref=src,
            dst_ref=dst,
            send_sem=self.send.at[k],
            recv_sem=self.recv.at[k],
            device_id=to,
            device_id_type=MESH,
        )
        copy.start()
        self.open.append(copy)
        return copy

    def drain(self):
        for copy in self.open:
            copy.wait_send()


FLOWS = 4
AR_WIRES = FLOWS * (4 + 6 + 6 + 7 + 7 + 6 + 6 + 5) + 14


def position():
    code, dp = lax.axis_index("code"), lax.axis_index("dp")
    return lax.div(dp, 2), lax.div(code, NZ), lax.rem(code, NZ), lax.rem(dp, 2)


def device(x, y, z, c):
    return (y * NZ + z, x * 2 + c)


class Ring:
    def __init__(self, wires, spot, right, left, size):
        self.w, self.p, self.n = wires, spot, size
        self.right, self.left = right, left
        self.h = size // 2

    def chunk(self, step):
        return lax.rem(self.p + step, 4) * self.n

    def scatter_start(self, acc, base, mid, edge):
        n, h, w = self.n, self.h, self.w
        self.acc, self.base, self.mid, self.edge = acc, base, mid, edge
        far, nxt, prv = (base + self.chunk(s) for s in (2, 1, 3))
        self.nxt, self.prv = nxt, prv
        self.far_a = w.start(acc.at[rows(far, h)], mid.at[0], self.right)
        self.far_b = w.start(acc.at[rows(far + h, h)], mid.at[1], self.left)
        self.near_b = w.start(acc.at[rows(nxt + h, h)], edge.at[0, pl.ds(h, h)], self.right)
        self.near_a = w.start(acc.at[rows(prv, h)], edge.at[1, pl.ds(0, h)], self.left)

    def scatter_mid(self):
        h, w, acc = self.h, self.w, self.acc
        self.far_a.wait_recv()
        here = rows(self.nxt, h)
        acc[here, :] = acc[here, :] + self.mid[0]
        self.pass_a = w.start(acc.at[here], self.edge.at[0, pl.ds(0, h)], self.right)
        self.far_b.wait_recv()
        here = rows(self.prv + h, h)
        acc[here, :] = acc[here, :] + self.mid[1]
        self.pass_b = w.start(acc.at[here], self.edge.at[1, pl.ds(h, h)], self.left)

    def scatter_end(self):
        for copy in (self.near_b, self.near_a, self.pass_a, self.pass_b):
            copy.wait_recv()
        mine = self.base + self.chunk(0)
        here = rows(mine, self.n)
        self.acc[here, :] = self.acc[here, :] + (self.edge[0] + self.edge[1])
        return mine

    def gather_start(self, out, base, cols):
        h, w = self.h, self.w
        self.out, self.base, self.cols = out, base, cols
        mine = base + self.chunk(0)
        first, second = (out.at[rows(mine + s, h), cols] for s in (0, h))
        self.right_a = w.start(first, first, self.right)
        self.left_b = w.start(second, second, self.left)
        self.right_b = w.start(second, second, self.right)
        self.left_a = w.start(first, first, self.left)

    def gather_mid(self):
        h, w, out = self.h, self.w, self.out
        self.right_a.wait_recv()
        part = out.at[rows(self.base + self.chunk(3), h), self.cols]
        self.on_a = w.start(part, part, self.right)
        self.left_b.wait_recv()
        part = out.at[rows(self.base + self.chunk(1) + h, h), self.cols]
        self.on_b = w.start(part, part, self.left)

    def gather_near(self):
        self.right_b.wait_recv()
        self.left_a.wait_recv()


ORDER = (2, 1, 3, 0)


class Flow:
    def __init__(self, q, wires, grads, out, bufs, tick, store):
        self.q, self.w, self.grads, self.out = q, wires, grads, out
        self.tick, self.store = tick, store
        acc, half, mid1, edge1, mid2, edge2, deep = bufs
        self.acc, self.half, self.deep = acc.at[q], half.at[q], deep.at[q]
        self.outer_bufs = mid1.at[q], edge1.at[q]
        self.inner_bufs = mid2.at[q], edge2.at[q]
        x, y, z, c = position()
        self.z, self.other = z, device(x, y, z, 1 - c)
        self.columns = [device(x, y, lax.rem(z + r, NZ), c) for r in range(1, NZ)]
        along_x = [x] + [device(lax.rem(x + s, NX), y, z, c) for s in (1, 3)]
        along_y = [y] + [device(x, lax.rem(y + s, NY), z, c) for s in (1, 3)]
        first, second = (along_x, along_y) if q % 2 == 0 else (along_y, along_x)
        self.outer, self.inner = Ring(wires, *first, 256), Ring(wires, *second, 64)
        place = (q % 2) * 256 + (q // 2) * LANES
        self.cols = pl.ds(pl.multiple_of(c * 512 + place, LANES), LANES)
        self.away = pl.ds(pl.multiple_of(512 - c * 512 + place, LANES), LANES)

    def swap(self):
        self.swaps = []
        for step in ORDER:
            here = rows(self.outer.chunk(step), 256)
            self.swaps.append(
                self.w.start(self.grads.at[here, self.away], self.half.at[here], self.other)
            )

    def back(self, start, size):
        part = self.out.at[rows(start, size), self.cols]
        self.backs.append(self.w.start(part, part, self.other))

    def steps(self):
        outer, inner, acc, z = self.outer, self.inner, self.acc, self.z
        for copy, step in zip(self.swaps, ORDER):
            here = rows(outer.chunk(step), 256)
            copy.wait_recv()
            acc[here, :] = self.grads[here, self.cols] + self.half[here, :]
            self.tick()
        outer.scatter_start(acc, 0, *self.outer_bufs)
        yield
        outer.scatter_mid()
        yield
        first = outer.scatter_end()
        inner.scatter_start(acc, first, *self.inner_bufs)
        yield
        inner.scatter_mid()
        yield
        second = inner.scatter_end()
        downs = []
        for r in range(1, NZ):
            part = acc.at[rows(second + lax.rem(z + r, NZ) * 8, 8)]
            downs.append(self.w.start(part, self.deep.at[r - 1], self.columns[r - 1]))
        yield
        for copy in downs:
            copy.wait_recv()
        here = rows(second + z * 8, 8)
        total = acc[here, :]
        for r in range(NZ - 1):
            total = total + self.deep[r]
        self.out[here, self.cols] = total
        part = self.out.at[here, self.cols]
        ups = [self.w.start(part, part, to) for to in self.columns]
        yield
        for copy in ups:
            copy.wait_recv()
        inner.gather_start(self.out, first, self.cols)
        yield
        inner.gather_mid()
        yield
        inner.gather_near()
        inner.on_a.wait_recv()
        inner.on_b.wait_recv()
        self.backs = []
        outer.gather_start(self.out, 0, self.cols)
        self.back(outer.chunk(0), 256)
        yield
        outer.gather_mid()
        yield
        outer.gather_near()
        self.back(outer.chunk(3), 256)
        self.back(outer.chunk(1), 256)
        yield
        outer.on_a.wait_recv()
        self.back(outer.chunk(2), 128)
        outer.on_b.wait_recv()
        self.back(outer.chunk(2) + 128, 128)
        self.store(self.cols)
        yield
        for copy in self.backs:
            copy.wait_recv()
        self.store(self.away)


def side_steps(wires, side, side_out, bufs):
    side0, side1, side2, side3 = bufs
    x, y, z, c = position()
    copy = wires.start(side, side0, device(x, y, z, 1 - c))
    yield
    copy.wait_recv()
    side1[x] = side[...] + side0[...]
    sides = [
        wires.start(side1.at[x], side1.at[x], device(lax.rem(x + r, NX), y, z, c))
        for r in range(1, NX)
    ]
    yield
    for copy in sides:
        copy.wait_recv()
    side2[y] = (side1[0] + side1[1]) + (side1[2] + side1[3])
    sides = [
        wires.start(side2.at[y], side2.at[y], device(x, lax.rem(y + r, NY), z, c))
        for r in range(1, NY)
    ]
    yield
    for copy in sides:
        copy.wait_recv()
    side3[z] = (side2[0] + side2[1]) + (side2[2] + side2[3])
    sides = [
        wires.start(side3.at[z], side3.at[z], device(x, y, lax.rem(z + r, NZ), c))
        for r in range(1, NZ)
    ]
    yield
    yield
    for copy in sides:
        copy.wait_recv()
    total = side3[0]
    for r in range(1, NZ):
        total = total + side3[r]
    side_out[...] = total


AR_BUFS = [
    pltpu.VMEM((FLOWS, 1024, LANES), F32),
    pltpu.VMEM((FLOWS, 1024, LANES), F32),
    pltpu.VMEM((FLOWS, 2, 128, LANES), F32),
    pltpu.VMEM((FLOWS, 2, 256, LANES), F32),
    pltpu.VMEM((FLOWS, 2, 32, LANES), F32),
    pltpu.VMEM((FLOWS, 2, 64, LANES), F32),
    pltpu.VMEM((FLOWS, 7, 8, LANES), F32),
    pltpu.VMEM((8, 256), F32),
    pltpu.VMEM((4, 8, 256), F32),
    pltpu.VMEM((4, 8, 256), F32),
    pltpu.VMEM((8, 8, 256), F32),
]


def greet(peers, sem):
    for peer in peers:
        pl.semaphore_signal(sem, inc=1, device_id=peer, device_id_type=MESH)


def owner_dp(group, forth=1):
    x, _, _, c = position()
    across = lax.rem(x + (NX + forth * (group // 2)), NX)
    return across * 2 + lax.rem(c + group % 2, 2)


class Exchange:
    def __init__(self, source, target, send, recv, forth):
        self.source, self.target, self.forth = source, target, forth
        self.send, self.recv, self.all = send, recv, []
        _, y, z, _ = position()
        self.y, self.z, self.me = y, z, y * NZ + z

    def start(self, group, begin=0, end=CODES):
        dp = owner_dp(group, self.forth)
        source, target = self.source.at[group], self.target.at[group]

        def copy(code, src, dst):
            return pltpu.make_async_remote_copy(
                src_ref=src,
                dst_ref=dst,
                send_sem=self.send.at[group],
                recv_sem=self.recv.at[group],
                device_id=(code, dp),
                device_id_type=MESH,
            )

        def one(i, carry):
            code = lax.rem(self.y + lax.div(i, NZ), NY) * NZ + lax.rem(self.z + lax.rem(i, NZ), NZ)
            copy(code, source.at[code], target.at[self.me]).start()
            return carry

        own = 1 if group == 0 else 0
        lax.fori_loop(max(own, begin), end, one, 0)
        if begin:
            return
        if own:
            self.target[group, self.me] = self.source[group, self.me]
        whole = pl.ds(0, CODES - own)
        near = self.y * NZ + lax.rem(self.z + 1, NZ)
        self.all.append(copy(near, source.at[whole], target.at[whole]))

    def arrived(self, group):
        self.all[group].wait_recv()

    def drain(self):
        for copy in self.all:
            copy.wait_send()


def dot(a, b):
    return jnp.dot(a, b, preferred_element_type=F32)


def halves(value):
    high = value.astype(BF16)
    low = (value - high.astype(F32)).astype(BF16)
    return jnp.concatenate([high, low], axis=1)


def joined(value):
    return value[:, :256] + value[:, 256:]


def upright(row):
    return jnp.transpose(jnp.broadcast_to(row, (128, row.shape[1])))


def iota(shape, dim):
    return lax.broadcasted_iota(jnp.int32, shape, dim)


def one_hot(condition):
    return jnp.where(condition, 1.0, 0.0).astype(BF16)


def slots_of(group, shape, dim):
    place = iota(shape, dim)
    slot = (place // CAP) * (GROUPS * CAP) + place % CAP + owner_dp(group) * CAP
    return slot.astype(F32)


def whole_kernel(
    codebook_h, weight_in_h, bias_in, weight_out_h, bias_out, latents_h, cotangent_h, owner, code,
    latent_grad_h, out_h, side_out,
    codebook, weight_in, weight_out, latents, cotangent, slot_col, values, send_a, recv_a, send_b,
    recv_b, ids_out, ids_in, slope, hidden_t, codebook_t, weight_out_t, projected, base, picks,
    code_low, grads, side, latent_grad, out,
    load, keep, ids_s, ids_r, a_s, a_r, b_s, b_r, near_a, near_b, wire_s, wire_r, *bufs,
):
    x, y, z, c = position()
    pairs = (
        (latents_h, latents), (cotangent_h, cotangent), (codebook_h, codebook),
        (weight_in_h, weight_in), (weight_out_h, weight_out),
    )
    loads = [pltpu.make_async_copy(src, dst, load.at[i]) for i, (src, dst) in enumerate(pairs)]
    for copy in loads:
        copy.start()
    barrier = pltpu.get_barrier_semaphore()
    row_peers = [
        device(lax.rem(x + r, NX), y, z, lax.rem(c + s, 2))
        for r in range(NX) for s in range(2) if r + s
    ]
    y_peers = [device(x, lax.rem(y + r, NY), z, c) for r in range(1, NY)]
    z_peers = [device(x, y, lax.rem(z + r, NZ), c) for r in range(1, NZ)]
    line_peers = row_peers + y_peers + z_peers
    greet(line_peers, barrier)

    owner_row = owner[...].astype(F32)
    code_row = code[...].astype(F32) + 1.0
    owner_col = upright(owner_row)
    lower = iota((128, 128), 0) < iota((128, 128), 1)
    ranks = []
    for i in range(8):
        name = owner_row[:, 128 * i : 128 * i + 128]
        count = jnp.where((owner_col[128 * i : 128 * i + 128] == name) & lower, 1.0, 0.0)
        for j in range(i):
            count += jnp.where(owner_col[128 * j : 128 * j + 128] == name, 1.0, 0.0)
        ranks.append(jnp.sum(count, axis=0, keepdims=True))
    rank_row = jnp.concatenate(ranks, axis=1)
    slot_row = owner_row * CAP + rank_row
    slot_col[...] = upright(slot_row)
    pl.semaphore_wait(barrier, len(line_peers))
    greet(row_peers, near_a)

    rank_col = upright(rank_row)
    code_col = upright(code_row)
    code_high = jnp.floor(code_col * (1.0 / 32))
    mine = rank_col == iota((1024, 128), 1).astype(F32)
    digits = jnp.concatenate(
        [
            jnp.where(mine, code_high, 0.0).astype(BF16),
            jnp.where(mine, code_col - 32.0 * code_high, 0.0).astype(BF16),
        ],
        axis=1,
    )
    place = iota((256, 1024), 0)
    group = place // CODES
    across = (x + group // 2) % NX * 2 + (c + group % 2) % 2
    named = dot(one_hot(owner_row == ((place % CODES) * GROUPS + across).astype(F32)), digits)
    named = named[:, :128] * 32.0 + named[:, 128:] - 1.0
    ids_out[...] = named.reshape(GROUPS, CODES, 1, 128)
    loads[0].wait()
    loads[1].wait()
    values[pl.ds(0, 1024), :] = halves(cotangent[...] - latents[...])
    pl.semaphore_wait(near_a, len(row_peers))
    greet(y_peers, near_b)

    names = Exchange(ids_out, ids_in, ids_s, ids_r, 1)
    forth = Exchange(send_a, recv_a, a_s, a_r, 1)
    answers = Exchange(send_b, recv_b, b_s, b_r, -1)
    for b in range(GROUPS):
        hot = one_hot(slot_row == slots_of(b, (256, 1024), 0))
        block = joined(dot(hot, values[pl.ds(0, 1024), :]))
        send_a[b] = block.reshape(CODES, CAP, 256)
        if b == 0:
            pl.semaphore_wait(near_b, len(y_peers))
            for k in range(GROUPS):
                names.start(k)
        forth.start(b)

    for copy in loads[2:]:
        copy.wait()
    weight_out_t[...] = jnp.transpose(weight_out[...].astype(F32)).astype(BF16)

    def forward(i, carry):
        here = rows(i * 256, 256)
        block = codebook[here, :]
        pre = dot(block, weight_in[...]) + bias_in[...]
        tangent = jnp.tanh(scale_gelu * (pre + cubic_term * pre * pre * pre))
        value = 0.5 * pre * (1.0 + tangent)
        slope[here, :] = 0.5 * (1.0 + tangent) + 0.5 * pre * (
            1.0 - tangent * tangent
        ) * scale_gelu * (1.0 + 3.0 * cubic_term * pre * pre)
        hidden = value.astype(BF16)
        cols = pl.ds(pl.multiple_of(i * 256, 256), 256)
        hidden_t[:, cols] = jnp.transpose(value).astype(BF16)
        codebook_t[:, cols] = jnp.transpose(block.astype(F32)).astype(BF16)
        block = dot(hidden, weight_out[...]) + bias_out[...]
        base[here, :] = block
        projected[here, :] = halves(block)
        return carry

    lax.fori_loop(0, 4, forward, 0)

    for b in range(GROUPS):
        names.arrived(b)
    ones = jnp.ones((256, 128), BF16)
    own = iota((256, 128), 0) % CAP == iota((256, 128), 1)
    for b in range(GROUPS):
        ids = ids_in[b]
        ids = jnp.broadcast_to(ids, (CODES, CAP, 128)).reshape(256, 128)
        ids = jnp.where(own, ids, 0.0)
        ids_col = jnp.sum(ids, axis=1, keepdims=True)
        ids_row = jnp.sum(jnp.transpose(ids), axis=0, keepdims=True)
        hot = one_hot(ids_col == iota((256, 1024), 1).astype(F32))
        send_b[b] = joined(dot(hot, projected[...])).reshape(CODES, CAP, 256)
        for i in range(4):
            hot = one_hot(ids_row == (iota((256, 256), 0) + 256 * i).astype(F32))
            picks[b, pl.ds(i * 256, 256), :] = hot
    for i in range(4):
        here = pl.ds(i * 256, 256)
        count = dot(picks[0, here, :], ones)
        for j in range(1, GROUPS):
            count += dot(picks[j, here, :], ones)
        base[here, :] = base[here, :] * jnp.concatenate([count, count], axis=1)

    for b in range(GROUPS):
        forth.arrived(b)
        if b == GROUPS - 1:
            answers.start(0)
        part = halves(recv_a[b].reshape(256, 256))
        for i in range(4):
            here = pl.ds(i * 256, 256)
            base[here, :] = base[here, :] + joined(dot(picks[b, here, :], part))
    code_low[...] = base[...].astype(BF16)
    side[...] = jnp.zeros((8, 256), F32)
    side[4:5, :] = jnp.sum(base[...], axis=0, keepdims=True)

    def gradient(b):
        cols = pl.ds(pl.multiple_of(b * 256, 256), 256)
        back = dot(code_low[...], weight_out_t[:, cols])
        low = (back * slope[:, cols]).astype(BF16)
        side[pl.ds(b, 1), :] = jnp.sum(low.astype(F32), axis=0, keepdims=True)
        grads[pl.ds(0, 768), cols] = dot(codebook_t[...], low)
        grads[pl.ds(768, 256), cols] = dot(hidden_t[rows(b * 256, 256), :], code_low[...])

    wires = Wires(wire_s, wire_r)
    chunks = [(k, i) for k in range(1, GROUPS) for i in range(0, CODES, PACE)]
    kept = []

    def tick():
        if chunks:
            k, i = chunks.pop(0)
            answers.start(k, i, i + PACE)

    def store(cols):
        copy = pltpu.make_async_copy(out.at[:, cols], out_h.at[:, cols], keep.at[len(kept)])
        copy.start()
        kept.append(copy)

    flows = [Flow(q, wires, grads, out, bufs[:7], tick, store) for q in range(FLOWS)]
    for q in range(2):
        gradient(2 - 2 * c + q)
    for flow in flows:
        flow.swap()
    for q in range(2):
        gradient(2 * c + q)

    def chosen(b):
        answers.arrived(b)
        part = halves(recv_b[b].reshape(256, 256))
        for i in range(4):
            here = pl.ds(i * 256, 256)
            slot, place = slot_col[here, :], slots_of(b, (256, 256), 1)
            hot = jnp.concatenate(
                [one_hot(slot == place[:, k * 128 : k * 128 + 128]) for k in range(2)], axis=1
            )
            total = joined(dot(hot, part))
            if b:
                total = total + latent_grad[here, :]
            if b == GROUPS - 1:
                total = cotangent[here, :] - 0.25 * (total - latents[here, :])
            latent_grad[here, :] = total

    picked = {11: [0], 12: [1], 13: [2], 14: [3], 15: [4], 16: [5], 17: [6], 18: [7]}
    running = []
    waiting = [side_steps(wires, side, side_out, bufs[7:])] + [flow.steps() for flow in flows]
    joins = {0: 3, 2: 2}
    turn = 0
    while running or waiting or turn <= max(picked):
        for _ in range(joins.get(turn, 0)):
            running.append(waiting.pop(0))
        for flow in list(running):
            if next(flow, flow) is flow:
                running.remove(flow)
            tick()
        for b in picked.get(turn, []):
            while chunks and chunks[0][0] <= b:
                tick()
            chosen(b)
        turn += 1
    copy = pltpu.make_async_copy(latent_grad, latent_grad_h, keep.at[len(kept)])
    copy.start()
    for copy in kept + [copy]:
        copy.wait()
    wires.drain()
    for exchange in (names, forth, answers):
        exchange.drain()
    assert wires.used == AR_WIRES, wires.used


def whole(codebook, weight_in, bias_in, weight_out, bias_out, latents, cotangent, owner, code):
    vmem, anywhere = (pl.BlockSpec(memory_space=m) for m in (pltpu.VMEM, pl.ANY))
    dma, plain = pltpu.SemaphoreType.DMA, pltpu.SemaphoreType.REGULAR
    scratch = [
        pltpu.VMEM((1024, 768), BF16),
        pltpu.VMEM((768, 1024), BF16),
        pltpu.VMEM((1024, 256), BF16),
        pltpu.VMEM((1024, 256), F32),
        pltpu.VMEM((1024, 256), F32),
        pltpu.VMEM((1024, 128), F32),
        pltpu.VMEM((1024, 512), BF16),
    ]
    scratch += [pltpu.VMEM((GROUPS, CODES, CAP, 256), F32)] * 4
    scratch += [pltpu.VMEM((GROUPS, CODES, 1, 128), F32)] * 2
    scratch += [
        pltpu.VMEM((1024, 1024), F32),
        pltpu.VMEM((1024, 1024), BF16),
        pltpu.VMEM((768, 1024), BF16),
        pltpu.VMEM((256, 1024), BF16),
        pltpu.VMEM((1024, 512), BF16),
        pltpu.VMEM((1024, 256), F32),
        pltpu.VMEM((GROUPS, 1024, 256), BF16),
        pltpu.VMEM((1024, 256), BF16),
        pltpu.VMEM((1024, 1024), F32),
        pltpu.VMEM((8, 256), F32),
        pltpu.VMEM((1024, 256), F32),
        pltpu.VMEM((1024, 1024), F32),
        dma((5,)),
        dma((2 * FLOWS + 1,)),
        *[dma((GROUPS,))] * 6,
        plain, plain,
        dma((AR_WIRES,)), dma((AR_WIRES,)),
    ]
    return pl.pallas_call(
        whole_kernel,
        out_shape=(
            jax.ShapeDtypeStruct((1024, 256), F32),
            jax.ShapeDtypeStruct((1024, 1024), F32),
            jax.ShapeDtypeStruct((8, 256), F32),
        ),
        in_specs=[anywhere, anywhere, vmem, anywhere, vmem, anywhere, anywhere, vmem, vmem],
        out_specs=(anywhere, anywhere, vmem),
        scratch_shapes=scratch + AR_BUFS,
        compiler_params=pltpu.CompilerParams(
            collective_id=1, has_side_effects=True, vmem_limit_bytes=60 * 2**20
        ),
    )(codebook, weight_in, bias_in, weight_out, bias_out, latents, cotangent, owner, code)


def finish_kernel(latent_grad, grads, side, latent_out, in_out, bias_in_out, w_out, bias_out, *bufs):
    part, whole_part, gets, puts = bufs
    pieces = []
    for j in range(2):
        here = pl.ds(j * 512, 512)
        pieces.append((latent_grad.at[here], part.at[here], [(part.at[here], latent_out.at[here])]))
    for j in range(6):
        here = pl.ds(j * 128, 128)
        pieces.append((grads.at[here], whole_part.at[here], [(whole_part.at[here], in_out.at[here])]))
    here = pl.ds(768, 256)
    pairs = [
        (whole_part.at[here, pl.ds(j * 256, 256)], w_out.at[pl.ds(j * 256, 256)]) for j in range(4)
    ]
    pieces.append((grads.at[here], whole_part.at[here], pairs))
    reads = [pltpu.make_async_copy(a, b, gets.at[i]) for i, (a, b, _) in enumerate(pieces)]
    for copy in reads:
        copy.start()
    for j in range(4):
        bias_in_out[:, j * 256 : j * 256 + 256] = side[j : j + 1, :]
    bias_out[...] = side[4:5, :]
    writes = []
    for copy, (_, _, pairs) in zip(reads, pieces):
        copy.wait()
        for a, b in pairs:
            writes.append(pltpu.make_async_copy(a, b, puts.at[len(writes)]))
            writes[-1].start()
    for copy in writes:
        copy.wait()


def finish(latent_grad, grads, side):
    vmem, anywhere = (pl.BlockSpec(memory_space=m) for m in (pltpu.VMEM, pl.ANY))
    return pl.pallas_call(
        finish_kernel,
        out_shape=tuple(
            jax.ShapeDtypeStruct(shape, F32)
            for shape in ((1024, 256), (768, 1024), (1, 1024), (1024, 256), (1, 256))
        ),
        in_specs=[anywhere, anywhere, vmem],
        out_specs=(anywhere, anywhere, vmem, anywhere, vmem),
        scratch_shapes=[
            pltpu.VMEM((1024, 256), F32),
            pltpu.VMEM((1024, 1024), F32),
            pltpu.SemaphoreType.DMA((9,)),
            pltpu.SemaphoreType.DMA((12,)),
        ],
        compiler_params=pltpu.CompilerParams(vmem_limit_bytes=60 * 2**20),
    )(latent_grad, grads, side)


def per_device(
    codebook, weight_in, bias_in, weight_out, bias_out, latents, cotangent, code_owner, code_row
):
    parts = whole(
        codebook, weight_in, bias_in[None], weight_out, bias_out[None], latents, cotangent,
        code_owner.reshape(1, 1024), code_row.reshape(1, 1024),
    )
    latent_grad, gw_in, gb_in, gw_out, gb_out = finish(*parts)
    return (latent_grad, gw_in, gb_in[0], gw_out, gb_out[0])


def solution(mesh):
    placed = (
        P(("code", "dp"), None),
        P(),
        P(),
        P(),
        P(),
        P(("code", "dp"), None),
        P(("code", "dp"), None),
        P(("code", "dp"), None),
        P(("code", "dp")),
    )
    return jax.shard_map(
        per_device,
        mesh=mesh,
        in_specs=placed,
        out_specs=(P(("code", "dp"), None), P(), P(), P(), P()),
        check_vma=False,
    )
```

time: 172 us -> 161 us (0.936)
  local copies, waits for them, and re-layouts: 10.4 us -> 0 us
    slice x3 -> x0, local copies, waits for them, and re-layouts: 6.52 us -> none  [the longest x1 3.97 us: per_device(): gw_in = grads[:768]]
    pallas_call x1, Pallas kernels: 161 us -> 154 us  [whole(): pl.pallas_call(whole_kernel, out_shape=(jax.ShapeDtypeStruct((1024, 256),...]
    pallas_call x0 -> x1, Pallas kernels: none -> 6.21 us  [finish(): pl.pallas_call(finish_kernel, out_shape=tuple((jax.ShapeDtypeStruct(shape...]
    unnamed x5 -> x0, local copies, waits for them, and re-layouts: 2.27 us -> none
where the time goes in v3:
time: 161 us
  Pallas kernels  160 us (99%)
    pallas_call x1, Pallas kernels, whole(): pl.pallas_call(whole_kernel, out_shape=(jax.ShapeDtypeStruct((1024, 256),...  154 us
    pallas_call x1, Pallas kernels, finish(): pl.pallas_call(finish_kernel, out_shape=tuple((jax.ShapeDtypeStruct(shape...  6.21 us

profile of v3, /device:TPU:1, one launch (start us, length us, event | category | flops | bytes accessed | tf_op | source)
XLA Modules:
  0.0 161.1 jit_solution(5746850553881668824)
XLA Ops:
  0.6 154.1 %shard_map.128 = (f32[1024,256]{1,0:T(8,128)}, f32[1024,1024]{1,0:T(8,128)}, f32[8,256]{1,0:T(8,128)}) custom-call(bf16[1024,768]{1,0:T(8,128)(2,1)} %codebook_h.1, bf16[768,1024]{1,0:T(8,128)(2,1)} %weight_in_h.1, f32[1,1024]{1,0:T(1,128)} %bitcast.6, bf16[1024,256]{1,0:T(8,128)(2,1)} %weight_out_h.1, f32[1,256]{1,0:T(1,128)} %bitcast.9, ...), custom_call_target="tpu_custom_call" | custom-call | tf_op jit(solution)/shard_map/pallas_call | solution.py:601
  154.7 6.2 %shard_map.129 = (f32[1024,256]{1,0:T(8,128)}, f32[768,1024]{1,0:T(8,128)}, f32[1,1024]{1,0:T(1,128)}, f32[1024,256]{1,0:T(8,128)}, f32[1,256]{1,0:T(1,128)}) custom-call(f32[1024,256]{1,0:T(8,128)} %get-tuple-element.13.latent_grad, f32[1024,1024]{1,0:T(8,128)} %get-tuple-element.14.grads, f32[8,256]{1,0:T(8,128)} %get-tuple-element.15.side), custom_call_target="tpu_custom_call" | custom-call | tf_op jit(solution)/shard_map/pallas_call | solution.py:649

commit v4 on v3

--- a/solution.py
+++ b/solution.py
@@ -13,7 +13,7 @@
 NX, NY, NZ = 4, 4, 8
 CAP, DEVICES, GROUPS, CODES = 8, 256, 8, 32
 PACE = 4
-LANES = 128
+LANES = 256
 F32, BF16 = jnp.float32, jnp.bfloat16
 
 
@@ -45,8 +45,8 @@
             copy.wait_send()
 
 
-FLOWS = 4
-AR_WIRES = FLOWS * (4 + 6 + 6 + 7 + 7 + 6 + 6 + 5) + 14
+FLOWS = 512 // LANES
+AR_WIRES = FLOWS * (4 + 6 + 3 + 7 + 7 + 3 + 6 + 5) + 14
 
 
 def position():
@@ -120,24 +120,57 @@
         self.left_a.wait_recv()
 
 
+class Direct:
+    def __init__(self, wires, spot, peers, size):
+        self.w, self.p, self.peers, self.n = wires, spot, peers, size
+
+    def chunk(self, step):
+        return lax.rem(self.p + step, 4) * self.n
+
+    def scatter_start(self, acc, base, edge):
+        self.acc, self.base, self.edge = acc, base, edge
+        self.copies = [
+            self.w.start(acc.at[rows(base + self.chunk(r), self.n)], edge.at[r - 1], to)
+            for r, to in zip((1, 2, 3), self.peers)
+        ]
+
+    def scatter_end(self):
+        for copy in self.copies:
+            copy.wait_recv()
+        mine = self.base + self.chunk(0)
+        here = rows(mine, self.n)
+        total = (self.edge[0] + self.edge[1]) + self.edge[2]
+        self.acc[here, :] = self.acc[here, :] + total
+        return mine
+
+    def gather_start(self, out, base, cols):
+        part = out.at[rows(base + self.chunk(0), self.n), cols]
+        self.copies = [self.w.start(part, part, to) for to in self.peers]
+
+    def gather_end(self):
+        for copy in self.copies:
+            copy.wait_recv()
+
+
 ORDER = (2, 1, 3, 0)
 
 
 class Flow:
-    def __init__(self, q, wires, grads, out, bufs, tick, store):
+    def __init__(self, q, wires, grads, out, bufs, tick):
         self.q, self.w, self.grads, self.out = q, wires, grads, out
-        self.tick, self.store = tick, store
-        acc, half, mid1, edge1, mid2, edge2, deep = bufs
+        self.tick = tick
+        acc, half, mid1, edge1, edge2, deep = bufs
         self.acc, self.half, self.deep = acc.at[q], half.at[q], deep.at[q]
         self.outer_bufs = mid1.at[q], edge1.at[q]
-        self.inner_bufs = mid2.at[q], edge2.at[q]
+        self.inner_buf = edge2.at[q]
         x, y, z, c = position()
         self.z, self.other = z, device(x, y, z, 1 - c)
         self.columns = [device(x, y, lax.rem(z + r, NZ), c) for r in range(1, NZ)]
-        along_x = [x] + [device(lax.rem(x + s, NX), y, z, c) for s in (1, 3)]
-        along_y = [y] + [device(x, lax.rem(y + s, NY), z, c) for s in (1, 3)]
+        along_x = x, [device(lax.rem(x + s, NX), y, z, c) for s in (1, 2, 3)]
+        along_y = y, [device(x, lax.rem(y + s, NY), z, c) for s in (1, 2, 3)]
         first, second = (along_x, along_y) if q % 2 == 0 else (along_y, along_x)
-        self.outer, self.inner = Ring(wires, *first, 256), Ring(wires, *second, 64)
+        self.outer = Ring(wires, first[0], first[1][0], first[1][2], 256)
+        self.inner = Direct(wires, *second, 64)
         place = (q % 2) * 256 + (q // 2) * LANES
         self.cols = pl.ds(pl.multiple_of(c * 512 + place, LANES), LANES)
         self.away = pl.ds(pl.multiple_of(512 - c * 512 + place, LANES), LANES)
@@ -166,9 +199,7 @@
         outer.scatter_mid()
         yield
         first = outer.scatter_end()
-        inner.scatter_start(acc, first, *self.inner_bufs)
-        yield
-        inner.scatter_mid()
+        inner.scatter_start(acc, first, self.inner_buf)
         yield
         second = inner.scatter_end()
         downs = []
@@ -190,11 +221,7 @@
             copy.wait_recv()
         inner.gather_start(self.out, first, self.cols)
         yield
-        inner.gather_mid()
-        yield
-        inner.gather_near()
-        inner.on_a.wait_recv()
-        inner.on_b.wait_recv()
+        inner.gather_end()
         self.backs = []
         outer.gather_start(self.out, 0, self.cols)
         self.back(outer.chunk(0), 256)
@@ -209,11 +236,9 @@
         self.back(outer.chunk(2), 128)
         outer.on_b.wait_recv()
         self.back(outer.chunk(2) + 128, 128)
-        self.store(self.cols)
         yield
         for copy in self.backs:
             copy.wait_recv()
-        self.store(self.away)
 
 
 def side_steps(wires, side, side_out, bufs):
@@ -258,8 +283,7 @@
     pltpu.VMEM((FLOWS, 1024, LANES), F32),
     pltpu.VMEM((FLOWS, 2, 128, LANES), F32),
     pltpu.VMEM((FLOWS, 2, 256, LANES), F32),
-    pltpu.VMEM((FLOWS, 2, 32, LANES), F32),
-    pltpu.VMEM((FLOWS, 2, 64, LANES), F32),
+    pltpu.VMEM((FLOWS, 3, 64, LANES), F32),
     pltpu.VMEM((FLOWS, 7, 8, LANES), F32),
     pltpu.VMEM((8, 256), F32),
     pltpu.VMEM((4, 8, 256), F32),
@@ -357,11 +381,11 @@
 
 def whole_kernel(
     codebook_h, weight_in_h, bias_in, weight_out_h, bias_out, latents_h, cotangent_h, owner, code,
-    latent_grad_h, out_h, side_out,
+    latent_grad, out, side_out,
     codebook, weight_in, weight_out, latents, cotangent, slot_col, values, send_a, recv_a, send_b,
-    recv_b, ids_out, ids_in, slope, hidden_t, codebook_t, weight_out_t, projected, base, picks,
-    code_low, grads, side, latent_grad, out,
-    load, keep, ids_s, ids_r, a_s, a_r, b_s, b_r, near_a, near_b, wire_s, wire_r, *bufs,
+    recv_b, ids_out, ids_mid, ids_sum, ids_in, slope, hidden_t, codebook_t, weight_out_t, projected, base, picks,
+    code_low, grads, side,
+    load, ids_s, ids_r, c_s, c_r, a_s, a_r, b_s, b_r, near_a, near_b, wire_s, wire_r, *bufs,
 ):
     x, y, z, c = position()
     pairs = (
@@ -396,12 +420,13 @@
     slot_row = owner_row * CAP + rank_row
     slot_col[...] = upright(slot_row)
     pl.semaphore_wait(barrier, len(line_peers))
-    greet(row_peers, near_a)
+    greet(y_peers, near_a)
 
     rank_col = upright(rank_row)
     code_col = upright(code_row)
     code_high = jnp.floor(code_col * (1.0 / 32))
-    mine = rank_col == iota((1024, 128), 1).astype(F32)
+    lane = iota((1024, 128), 1)
+    mine = (rank_col == (lane % CAP).astype(F32)) & (lane < GROUPS * CAP)
     digits = jnp.concatenate(
         [
             jnp.where(mine, code_high, 0.0).astype(BF16),
@@ -413,26 +438,45 @@
     group = place // CODES
     across = (x + group // 2) % NX * 2 + (c + group % 2) % 2
     named = dot(one_hot(owner_row == ((place % CODES) * GROUPS + across).astype(F32)), digits)
-    named = named[:, :128] * 32.0 + named[:, 128:] - 1.0
-    ids_out[...] = named.reshape(GROUPS, CODES, 1, 128)
+    named = named[:, :128] * 32.0 + named[:, 128:]
+    ours = iota((256, 128), 1) // CAP == iota((256, 128), 0) // CODES
+    ids_out[...] = jnp.where(ours, named, 0.0).reshape(GROUPS, CODES, 1, 128)
+    aside = []
+    for b in range(1, GROUPS):
+        aside.append(
+            pltpu.make_async_remote_copy(
+                src_ref=ids_out.at[b],
+                dst_ref=ids_mid.at[b],
+                send_sem=ids_s.at[b],
+                recv_sem=ids_r.at[b],
+                device_id=(y * NZ + z, owner_dp(b)),
+                device_id_type=MESH,
+            )
+        )
+        aside[-1].start()
     loads[0].wait()
     loads[1].wait()
     values[pl.ds(0, 1024), :] = halves(cotangent[...] - latents[...])
-    pl.semaphore_wait(near_a, len(row_peers))
-    greet(y_peers, near_b)
-
-    names = Exchange(ids_out, ids_in, ids_s, ids_r, 1)
+    pl.semaphore_wait(near_a, len(y_peers))
+    greet(row_peers, near_b)
+
+    names = Exchange(ids_sum, ids_in, c_s, c_r, 1)
     forth = Exchange(send_a, recv_a, a_s, a_r, 1)
     answers = Exchange(send_b, recv_b, b_s, b_r, -1)
     for b in range(GROUPS):
         hot = one_hot(slot_row == slots_of(b, (256, 1024), 0))
         block = joined(dot(hot, values[pl.ds(0, 1024), :]))
         send_a[b] = block.reshape(CODES, CAP, 256)
-        if b == 0:
-            pl.semaphore_wait(near_b, len(y_peers))
-            for k in range(GROUPS):
-                names.start(k)
+        if b == 1:
+            pl.semaphore_wait(near_b, len(row_peers))
         forth.start(b)
+        if b == 1:
+            total = ids_out[0]
+            for k in range(1, GROUPS):
+                aside[k - 1].wait_recv()
+                total = total + ids_mid[k]
+            ids_sum[0] = total
+            names.start(0)
 
     for copy in loads[2:]:
         copy.wait()
@@ -458,20 +502,19 @@
 
     lax.fori_loop(0, 4, forward, 0)
 
+    names.arrived(0)
+    ones = jnp.ones((256, 128), BF16)
     for b in range(GROUPS):
-        names.arrived(b)
-    ones = jnp.ones((256, 128), BF16)
-    own = iota((256, 128), 0) % CAP == iota((256, 128), 1)
-    for b in range(GROUPS):
-        ids = ids_in[b]
+        ids = ids_in[0]
+        own = iota((256, 128), 0) % CAP + b * CAP == iota((256, 128), 1)
         ids = jnp.broadcast_to(ids, (CODES, CAP, 128)).reshape(256, 128)
         ids = jnp.where(own, ids, 0.0)
         ids_col = jnp.sum(ids, axis=1, keepdims=True)
         ids_row = jnp.sum(jnp.transpose(ids), axis=0, keepdims=True)
-        hot = one_hot(ids_col == iota((256, 1024), 1).astype(F32))
+        hot = one_hot(ids_col == (iota((256, 1024), 1) + 1).astype(F32))
         send_b[b] = joined(dot(hot, projected[...])).reshape(CODES, CAP, 256)
         for i in range(4):
-            hot = one_hot(ids_row == (iota((256, 256), 0) + 256 * i).astype(F32))
+            hot = one_hot(ids_row == (iota((256, 256), 0) + (256 * i + 1)).astype(F32))
             picks[b, pl.ds(i * 256, 256), :] = hot
     for i in range(4):
         here = pl.ds(i * 256, 256)
@@ -501,24 +544,20 @@
         grads[pl.ds(768, 256), cols] = dot(hidden_t[rows(b * 256, 256), :], code_low[...])
 
     wires = Wires(wire_s, wire_r)
-    chunks = [(k, i) for k in range(1, GROUPS) for i in range(0, CODES, PACE)]
-    kept = []
+    chunks = []
 
     def tick():
         if chunks:
             k, i = chunks.pop(0)
             answers.start(k, i, i + PACE)
 
-    def store(cols):
-        copy = pltpu.make_async_copy(out.at[:, cols], out_h.at[:, cols], keep.at[len(kept)])
-        copy.start()
-        kept.append(copy)
-
-    flows = [Flow(q, wires, grads, out, bufs[:7], tick, store) for q in range(FLOWS)]
+    flows = [Flow(q, wires, grads, out, bufs[:6], tick) for q in range(FLOWS)]
     for q in range(2):
         gradient(2 - 2 * c + q)
     for flow in flows:
         flow.swap()
+    for k in range(1, GROUPS):
+        answers.start(k)
     for q in range(2):
         gradient(2 * c + q)
 
@@ -538,10 +577,10 @@
                 total = cotangent[here, :] - 0.25 * (total - latents[here, :])
             latent_grad[here, :] = total
 
-    picked = {11: [0], 12: [1], 13: [2], 14: [3], 15: [4], 16: [5], 17: [6], 18: [7]}
+    picked = {8: [0], 9: [1, 2], 10: [3, 4], 11: [5, 6], 12: [7]}
     running = []
-    waiting = [side_steps(wires, side, side_out, bufs[7:])] + [flow.steps() for flow in flows]
-    joins = {0: 3, 2: 2}
+    waiting = [side_steps(wires, side, side_out, bufs[6:])] + [flow.steps() for flow in flows]
+    joins = {0: 3}
     turn = 0
     while running or waiting or turn <= max(picked):
         for _ in range(joins.get(turn, 0)):
@@ -555,13 +594,11 @@
                 tick()
             chosen(b)
         turn += 1
-    copy = pltpu.make_async_copy(latent_grad, latent_grad_h, keep.at[len(kept)])
-    copy.start()
-    for copy in kept + [copy]:
-        copy.wait()
     wires.drain()
     for exchange in (names, forth, answers):
         exchange.drain()
+    for copy in aside:
+        copy.wait_send()
     assert wires.used == AR_WIRES, wires.used
 
 
@@ -579,6 +616,7 @@
     ]
     scratch += [pltpu.VMEM((GROUPS, CODES, CAP, 256), F32)] * 4
     scratch += [pltpu.VMEM((GROUPS, CODES, 1, 128), F32)] * 2
+    scratch += [pltpu.VMEM((1, CODES, 1, 128), F32)] * 2
     scratch += [
         pltpu.VMEM((1024, 1024), F32),
         pltpu.VMEM((1024, 1024), BF16),
@@ -590,57 +628,43 @@
         pltpu.VMEM((1024, 256), BF16),
         pltpu.VMEM((1024, 1024), F32),
         pltpu.VMEM((8, 256), F32),
-        pltpu.VMEM((1024, 256), F32),
-        pltpu.VMEM((1024, 1024), F32),
         dma((5,)),
-        dma((2 * FLOWS + 1,)),
-        *[dma((GROUPS,))] * 6,
+        *[dma((GROUPS,))] * 8,
         plain, plain,
         dma((AR_WIRES,)), dma((AR_WIRES,)),
     ]
     return pl.pallas_call(
         whole_kernel,
         out_shape=(
-            jax.ShapeDtypeStruct((1024, 256), F32),
-            jax.ShapeDtypeStruct((1024, 1024), F32),
-            jax.ShapeDtypeStruct((8, 256), F32),
+            pltpu.VMEM((1024, 256), F32),
+            pltpu.VMEM((1024, 1024), F32),
+            pltpu.VMEM((8, 256), F32),
         ),
         in_specs=[anywhere, anywhere, vmem, anywhere, vmem, anywhere, anywhere, vmem, vmem],
-        out_specs=(anywhere, anywhere, vmem),
+        out_specs=(vmem, vmem, vmem),
         scratch_shapes=scratch + AR_BUFS,
         compiler_params=pltpu.CompilerParams(
-            collective_id=1, has_side_effects=True, vmem_limit_bytes=60 * 2**20
+            collective_id=1, has_side_effects=True, vmem_limit_bytes=52 * 2**20
         ),
     )(codebook, weight_in, bias_in, weight_out, bias_out, latents, cotangent, owner, code)
 
 
-def finish_kernel(latent_grad, grads, side, latent_out, in_out, bias_in_out, w_out, bias_out, *bufs):
-    part, whole_part, gets, puts = bufs
-    pieces = []
-    for j in range(2):
-        here = pl.ds(j * 512, 512)
-        pieces.append((latent_grad.at[here], part.at[here], [(part.at[here], latent_out.at[here])]))
-    for j in range(6):
-        here = pl.ds(j * 128, 128)
-        pieces.append((grads.at[here], whole_part.at[here], [(whole_part.at[here], in_out.at[here])]))
-    here = pl.ds(768, 256)
-    pairs = [
-        (whole_part.at[here, pl.ds(j * 256, 256)], w_out.at[pl.ds(j * 256, 256)]) for j in range(4)
+def finish_kernel(latent_grad, grads, side, latent_out, in_out, bias_in_out, w_out, bias_out, sems):
+    copies = [
+        pltpu.make_async_copy(latent_grad, latent_out, sems.at[0]),
+        pltpu.make_async_copy(grads.at[pl.ds(0, 768)], in_out, sems.at[1]),
     ]
-    pieces.append((grads.at[here], whole_part.at[here], pairs))
-    reads = [pltpu.make_async_copy(a, b, gets.at[i]) for i, (a, b, _) in enumerate(pieces)]
-    for copy in reads:
+    for j in range(4):
+        piece = pl.ds(j * 256, 256)
+        copies.append(
+            pltpu.make_async_copy(grads.at[pl.ds(768, 256), piece], w_out.at[piece], sems.at[2 + j])
+        )
+    for copy in copies:
         copy.start()
     for j in range(4):
         bias_in_out[:, j * 256 : j * 256 + 256] = side[j : j + 1, :]
     bias_out[...] = side[4:5, :]
-    writes = []
-    for copy, (_, _, pairs) in zip(reads, pieces):
-        copy.wait()
-        for a, b in pairs:
-            writes.append(pltpu.make_async_copy(a, b, puts.at[len(writes)]))
-            writes[-1].start()
-    for copy in writes:
+    for copy in copies:
         copy.wait()
 
 
@@ -652,15 +676,10 @@
             jax.ShapeDtypeStruct(shape, F32)
             for shape in ((1024, 256), (768, 1024), (1, 1024), (1024, 256), (1, 256))
         ),
-        in_specs=[anywhere, anywhere, vmem],
+        in_specs=[vmem, vmem, vmem],
         out_specs=(anywhere, anywhere, vmem, anywhere, vmem),
-        scratch_shapes=[
-            pltpu.VMEM((1024, 256), F32),
-            pltpu.VMEM((1024, 1024), F32),
-            pltpu.SemaphoreType.DMA((9,)),
-            pltpu.SemaphoreType.DMA((12,)),
-        ],
-        compiler_params=pltpu.CompilerParams(vmem_limit_bytes=60 * 2**20),
+        scratch_shapes=[pltpu.SemaphoreType.DMA((6,))],
+        compiler_params=pltpu.CompilerParams(vmem_limit_bytes=16 * 2**20),
     )(latent_grad, grads, side)
 
 

time: 161 us -> 148 us (0.919)
  Pallas kernels: 160 us -> 147 us
    pallas_call x1, Pallas kernels: 154 us -> 144 us  [whole(): pl.pallas_call(whole_kernel, out_shape=(pltpu.VMEM((1024, 256), F32), plt...]
    pallas_call x1, Pallas kernels: 6.21 us -> 2.97 us  [finish(): pl.pallas_call(finish_kernel, out_shape=tuple((jax.ShapeDtypeStruct(shape...]
where the time goes in v4:
time: 148 us
  Pallas kernels  147 us (99%)
    pallas_call x1, Pallas kernels, whole(): pl.pallas_call(whole_kernel, out_shape=(pltpu.VMEM((1024, 256), F32), plt...  144 us
    pallas_call x1, Pallas kernels, finish(): pl.pallas_call(finish_kernel, out_shape=tuple((jax.ShapeDtypeStruct(shape...  2.97 us

profile of v4, /device:TPU:1, one launch (start us, length us, event | category | flops | bytes accessed | tf_op | source)
XLA Modules:
  0.0 147.7 jit_solution(15272470029852015680)
XLA Ops:
  0.6 143.9 %shard_map.128 = (f32[1024,256]{1,0:T(8,128)S(1)}, f32[1024,1024]{1,0:T(8,128)S(1)}, f32[8,256]{1,0:T(8,128)S(1)}) custom-call(bf16[1024,768]{1,0:T(8,128)(2,1)} %codebook_h.1, bf16[768,1024]{1,0:T(8,128)(2,1)} %weight_in_h.1, f32[1,1024]{1,0:T(1,128)} %bitcast.6, bf16[1024,256]{1,0:T(8,128)(2,1)} %weight_out_h.1, f32[1,256]{1,0:T(1,128)} %bitcast.9, ...), custom_call_target="tpu_custom_call" | custom-call | tf_op jit(solution)/shard_map/pallas_call | solution.py:636
  144.5 3.0 %shard_map.129 = (f32[1024,256]{1,0:T(8,128)}, f32[768,1024]{1,0:T(8,128)}, f32[1,1024]{1,0:T(1,128)}, f32[1024,256]{1,0:T(8,128)}, f32[1,256]{1,0:T(1,128)}) custom-call(f32[1024,256]{1,0:T(8,128)S(1)} %get-tuple-element.13.latent_grad, f32[1024,1024]{1,0:T(8,128)S(1)} %get-tuple-element.14.grads, f32[8,256]{1,0:T(8,128)S(1)} %get-tuple-element.15.side), custom_call_target="tpu_custom_call" | custom-call | tf_op jit(solution)/shard_map/pallas_call | solution.py:673

commit v5 on v4

--- a/solution.py
+++ b/solution.py
@@ -525,8 +525,8 @@
 
     for b in range(GROUPS):
         forth.arrived(b)
-        if b == GROUPS - 1:
-            answers.start(0)
+        if 4 <= b < 7:
+            answers.start(b - 4)
         part = halves(recv_a[b].reshape(256, 256))
         for i in range(4):
             here = pl.ds(i * 256, 256)
@@ -556,7 +556,7 @@
         gradient(2 - 2 * c + q)
     for flow in flows:
         flow.swap()
-    for k in range(1, GROUPS):
+    for k in range(3, GROUPS):
         answers.start(k)
     for q in range(2):
         gradient(2 * c + q)

time: 148 us -> 145 us (0.980)
  Pallas kernels: 147 us -> 144 us
    pallas_call x1, Pallas kernels: 144 us -> 141 us  [whole(): pl.pallas_call(whole_kernel, out_shape=(pltpu.VMEM((1024, 256), F32), plt...]
where the time goes in v5:
time: 145 us; the launch traced here: 144 us
  Pallas kernels  144 us (99%)
    pallas_call x1, Pallas kernels, whole(): pl.pallas_call(whole_kernel, out_shape=(pltpu.VMEM((1024, 256), F32), plt...  141 us
    pallas_call x1, Pallas kernels, finish(): pl.pallas_call(finish_kernel, out_shape=tuple((jax.ShapeDtypeStruct(shape...  2.97 us

profile of v5, /device:TPU:1, one launch (start us, length us, event | category | flops | bytes accessed | tf_op | source)
XLA Modules:
  0.0 144.5 jit_solution(10972967137675818265)
XLA Ops:
  0.6 140.7 %shard_map.128 = (f32[1024,256]{1,0:T(8,128)S(1)}, f32[1024,1024]{1,0:T(8,128)S(1)}, f32[8,256]{1,0:T(8,128)S(1)}) custom-call(bf16[1024,768]{1,0:T(8,128)(2,1)} %codebook_h.1, bf16[768,1024]{1,0:T(8,128)(2,1)} %weight_in_h.1, f32[1,1024]{1,0:T(1,128)} %bitcast.6, bf16[1024,256]{1,0:T(8,128)(2,1)} %weight_out_h.1, f32[1,256]{1,0:T(1,128)} %bitcast.9, ...), custom_call_target="tpu_custom_call" | custom-call | tf_op jit(solution)/shard_map/pallas_call | solution.py:636
  141.3 3.0 %shard_map.129 = (f32[1024,256]{1,0:T(8,128)}, f32[768,1024]{1,0:T(8,128)}, f32[1,1024]{1,0:T(1,128)}, f32[1024,256]{1,0:T(8,128)}, f32[1,256]{1,0:T(1,128)}) custom-call(f32[1024,256]{1,0:T(8,128)S(1)} %get-tuple-element.13.latent_grad, f32[1024,1024]{1,0:T(8,128)S(1)} %get-tuple-element.14.grads, f32[8,256]{1,0:T(8,128)S(1)} %get-tuple-element.15.side), custom_call_target="tpu_custom_call" | custom-call | tf_op jit(solution)/shard_map/pallas_call | solution.py:673
